TPU v7x, 32 devices: a whole 2x2x4 slice. The times are simulated.
32 devices in a mesh: groups: 2 (over x), tiles: 16 (over z, y, core).
Axes of the slice: x: 2, y: 2, z: 4, core: 2. Of those that a mesh axis runs over, the one named last changes fastest.
Arguments:
- estimate: float32 [768, 16, 512], P(('groups', 'tiles')), parts along dimension 0, may hold values from 0.25 to 4
- observed: bfloat16 [32, 16, 18, 16, 512], P(('groups', 'tiles')), parts along dimension 0, may hold values from 0.25 to 4
- item_tile: int32 [768, 6], P(('groups', 'tiles')), parts along dimension 0, may hold values from 0 to 15, all different within a row; in each aligned block of 24 rows (0 to 23, 24 to 47, ...) at most 18 rows name the same one
- psf_sigma: float32 [6, 3], replicated, may hold values from 0.7 to 3
- view_offsets: int32 [6, 3], replicated, may hold values from -6 to 6
Outputs:
- updated: float32 [768, 16, 512], P(('groups', 'tiles')), parts along dimension 0
There are 2 independent parts, one for each index of `groups`. A program takes and returns all parts, laid end to end along the dimension named above; an argument that names none is the same for every part. Nothing has to cross between parts.
Inputs may be any that keep to these rules, and one draw needn't show every extreme that they name: `item_tile`: the 6 tiles of a row differ; among the 24 rows of one device no tile is named more than 18 times, a bound that some block reaches.
All inputs are finite; a program needn't handle non-finite values.
Results may differ from a plain program's by a relative error of at most 0.0084.
Values may be sent and summed in bfloat16 or wider, within the bound.
No kernel may reach another device: no remote copies, remote signals or barrier semaphores. Data moves between devices by JAX's collectives and lax.ppermute only.
A program may use at most 192 MiB of HBM per device.

v0:
```python
import jax
import jax.numpy as jnp
from jax import lax
from jax.sharding import PartitionSpec as P

BX = 32
BY = 16


tap_reach = 15


def circulant(spread, offset, kernel_length):
    positions = jnp.arange(kernel_length, dtype=jnp.int32)
    distance_raw = positions[None, None, :] - positions[None, :, None] - offset[:, None, None]
    half_kernel_length = kernel_length // 2
    distance = jnp.mod(distance_raw + half_kernel_length, kernel_length) - half_kernel_length
    distance_f = distance.astype(jnp.float32)
    kernel_weight = jnp.where(
        jnp.abs(distance) <= tap_reach,
        jnp.exp(-distance_f * distance_f / (2.0 * spread[:, None, None] ** 2)),
        jnp.float32(0.0),
    )
    return (kernel_weight / jnp.sum(kernel_weight, axis=2, keepdims=True)).astype(jnp.bfloat16)


def select_rows(indicator_matrix, owner_lookup):
    return jnp.einsum(
        "ln,ntr->ltr", indicator_matrix, owner_lookup, preferred_element_type=jnp.float32
    ).astype(jnp.bfloat16)


def correction_items(estimates, observations, view_ids, tables):
    z_table, y_table, x_table = tables
    indicator_matrix = (
        view_ids[:, None] == jnp.arange(x_table.shape[0], dtype=jnp.int32)[None, :]
    ).astype(jnp.bfloat16)
    z_matrix = select_rows(indicator_matrix, z_table)
    y_matrix = select_rows(indicator_matrix, y_table)
    x_matrix = select_rows(indicator_matrix, x_table)
    section = jnp.einsum(
        "szyk,sxk->szyx", estimates, x_matrix, preferred_element_type=jnp.float32
    ).astype(jnp.bfloat16)
    section = jnp.einsum(
        "szkx,syk->szyx", section, y_matrix, preferred_element_type=jnp.float32
    ).astype(jnp.bfloat16)
    blurred = jnp.einsum("skyx,szk->szyx", section, z_matrix, preferred_element_type=jnp.float32)
    quotient = (observations.astype(jnp.float32) / blurred).astype(jnp.bfloat16)
    section = jnp.einsum(
        "skyx,skz->szyx", quotient, z_matrix, preferred_element_type=jnp.float32
    ).astype(jnp.bfloat16)
    section = jnp.einsum(
        "szkx,sky->szyx", section, y_matrix, preferred_element_type=jnp.float32
    ).astype(jnp.bfloat16)
    return jnp.einsum(
        "szyk,skx->szyx", section, x_matrix, preferred_element_type=jnp.float32
    ).astype(jnp.bfloat16)


def per_device(estimate, observed, item_tile, psf_sigma, view_offsets):
    blocks, depth_cells, plane_cells = estimate.shape
    row_cells = BY
    col_cells = BX
    view_count = item_tile.shape[1]
    tile_count = lax.axis_size("tiles")
    slot_count = observed.shape[2]
    block_shape = (depth_cells, row_cells, col_cells)
    tables = (
        circulant(psf_sigma[:, 0], view_offsets[:, 0], depth_cells),
        circulant(psf_sigma[:, 1], view_offsets[:, 1], row_cells),
        circulant(psf_sigma[:, 2], view_offsets[:, 2], col_cells),
    )
    flat_tiles = item_tile.reshape(-1)
    hit_table = (flat_tiles[:, None] == jnp.arange(tile_count, dtype=jnp.int32)[None, :]).astype(
        jnp.int32
    )
    before = jnp.cumsum(hit_table, axis=0) - hit_table
    slot_rank = jnp.sum(before * hit_table, axis=1)
    target = flat_tiles * slot_count + slot_rank
    view_ids = jnp.tile(jnp.arange(view_count, dtype=jnp.int32), blocks)
    est_bf = estimate.astype(jnp.bfloat16).reshape((blocks,) + block_shape)
    item_est = jnp.repeat(est_bf, view_count, axis=0)
    arrived = lax.all_to_all(observed[0], "tiles", split_axis=0, concat_axis=0, tiled=True)
    gathered = arrived.reshape((tile_count * slot_count,) + block_shape)[target]
    corrections = correction_items(item_est, gathered, view_ids, tables)
    factor = jnp.prod(
        corrections.reshape((blocks, view_count) + block_shape).astype(jnp.float32), axis=1
    )
    return estimate * factor.reshape(blocks, depth_cells, plane_cells)


def solution(mesh):
    return jax.shard_map(
        per_device,
        mesh=mesh,
        in_specs=(
            P(("groups", "tiles"), None, None),
            P(("groups", "tiles"), None, None, None, None),
            P(("groups", "tiles"), None),
            P(),
            P(),
        ),
        out_specs=P(("groups", "tiles"), None, None),
        check_vma=False,
    )
```

profile of v0, /device:TPU:15, one launch (start us, length us, event | category | flops | bytes accessed | tf_op | source)
XLA Modules:
  0.0 199.8 jit_solution(13879577120057665026)
XLA Ops:
  0.0 0.0 copy-start
  0.0 6.7 %all-to-all-start = ((bf16[16,18,16,512]{3,2,1,0:T(8,128)(2,1)}), bf16[16,18,16,512]{3,2,1,0:T(8,128)(2,1)}, u32[]{:S(2)}, u32[]{:S(2)}) async-start(bf16[16,18,16,512]{3,2,1,0:T(8,128)(2,1)} %bitcast.67), calls=%async_computation | async-start | bytes 9437184 | tf_op jit(solution)/shard_map/all_to_all | solution.py:83
  6.7 0.1 eq.58
  6.9 0.3 fusion.42
  7.2 0.7 fusion.22
  7.9 1.1 copy.39
  8.9 0.3 fusion.46
  9.2 0.3 fusion.23
  9.5 0.5 copy.43
  10.1 0.3 fusion.24
  10.4 1.3 copy.42
  11.7 0.1 copy.26
  11.8 0.1 copy.25
  11.9 0.1 mul.72
  12.0 0.1 eq.62
  12.1 0.6 reduce-window.6
  12.7 0.2 slice_reduce_fusion
  12.9 0.8 convert_element_type.82
  13.7 2.0 %reshape.132 = bf16[24,16,16,32]{3,2,1,0:T(8,128)(2,1)S(1)} reshape(bf16[24,16,512]{2,1,0:T(8,128)(2,1)} %convert_element_type.82) | data formatting | bytes 786432 | tf_op jit(solution)/shard_map/reshape | solution.py:81
  15.8 2.3 %broadcast_in_dim.13 = bf16[24,6,16,16,32]{4,3,2,1,0:T(8,128)(2,1)S(1)} broadcast(bf16[24,16,16,32]{3,2,1,0:T(8,128)(2,1)S(1)} %reshape.132), dimensions={0,2,3,4} | broadcast | bytes 2752512 | tf_op jit(solution)/shard_map/broadcast_in_dim | solution.py:82
  18.1 5.0 %convert_bitcast_fusion.1 = bf16[144,16,16,32]{3,2,1,0:T(8,128)(2,1)} fusion(bf16[144,32,32,1]{2,1,3,0:T(8,128)(2,1)S(1)} %copy.39, bf16[144,16,16,32]{3,2,1,0:T(8,128)(2,1)S(1)} %bitcast.65), kind=kOutput, calls=%fused_computation.11 | convolution fusion | flops 76677120 | bytes 5013504 | tf_op jit(solution)/shard_map/szyk,sxk->szyx/dot_general | solution.py:41
  23.1 21.1 %copy.32 = bf16[144,16,16,32]{2,1,3,0:T(8,128)(2,1)} copy(bf16[144,16,16,32]{3,2,1,0:T(8,128)(2,1)} %convert_bitcast_fusion.1) | data formatting | bytes 4718592 | tf_op jit(solution)/shard_map/convert_element_type | solution.py:43
  44.3 0.1 bitcast_bitcast_fusion
  44.4 49.1 %convert_bitcast_fusion = bf16[144,16,16,32]{1,2,3,0:T(8,128)(2,1)} fusion(bf16[144,16,16,1]{1,2,3,0:T(8,128)(2,1)S(1)} %copy.43, bf16[144,16,16,32]{2,1,3,0:T(8,128)(2,1)} %copy.32), kind=kOutput, calls=%fused_computation.5 | convolution fusion | flops 38928384 | bytes 4792320 | tf_op jit(solution)/shard_map/szkx,syk->szyx/dot_general | solution.py:44
  93.5 16.9 %all-to-all-done = bf16[16,18,16,512]{3,2,1,0:T(8,128)(2,1)} async-done(((bf16[16,18,16,512]{3,2,1,0:T(8,128)(2,1)}), bf16[16,18,16,512]{3,2,1,0:T(8,128)(2,1)}, u32[]{:S(2)}, u32[]{:S(2)}) %all-to-all-start) | async-done | bytes 4718624 | tf_op jit(solution)/shard_map/all_to_all | solution.py:83
  110.4 21.4 %reshape.129 = bf16[288,16,16,32]{3,2,1,0:T(8,128)(2,1)} reshape(bf16[16,18,16,512]{3,2,1,0:T(8,128)(2,1)} %all-to-all-done) | data formatting | bytes 9437184 | tf_op jit(solution)/shard_map/reshape | solution.py:84
  131.8 13.7 %gather_fusion = bf16[144,16,16,32]{3,2,1,0:T(8,128)(2,1)} fusion(bf16[288,16,16,32]{3,2,1,0:T(8,128)(2,1)} %reshape.129, s32[1024]{0:T(1024)S(1)} %pad_clamp_fusion), kind=kCustom, calls=%fused_computation | custom fusion | bytes 4719168 | tf_op jit(solution)/shard_map/gather | solution.py:84
  145.6 32.8 %fusion.15 = bf16[144,16,16,32]{3,1,2,0:T(8,128)(2,1)} fusion(bf16[144,16,16,1]{1,2,3,0:T(8,128)(2,1)S(1)} %copy-done.1, bf16[144,16,16,32]{3,2,1,0:T(8,128)(2,1)} %gather_fusion, bf16[144,16,16,32]{1,2,3,0:T(8,128)(2,1)} %convert_bitcast_fusion), kind=kOutput, calls=%fused_computation.14 | convolution fusion | flops 80216064 | bytes 7151616 | tf_op jit(solution)/shard_map/skyx,skz->szyx/dot_general | solution.py:49
  178.4 10.9 %fusion.12 = bf16[144,16,16,32]{3,2,1,0:T(8,128)(2,1)} fusion(bf16[144,32,32,1]{2,1,3,0:T(8,128)(2,1)S(1)} %copy.39, bf16[144,16,16,1]{1,2,3,0:T(8,128)(2,1)S(1)} %copy.43, bf16[144,16,16,32]{3,1,2,0:T(8,128)(2,1)} %fusion.15), kind=kOutput, calls=%fused_computation.13 | convolution fusion | flops 115605504 | bytes 5087232 | tf_op jit(solution)/shard_map/szyk,skx->szyx/dot_general | solution.py:55
  189.4 6.0 %convert_reduce_fusion = f32[24,16,16,32]{3,2,1,0:T(8,128)S(1)} fusion(bf16[24,6,16,16,32]{4,3,2,1,0:T(8,128)(2,1)} %bitcast.66), kind=kLoop, calls=%fused_computation.1 | loop fusion | flops 2162688 | bytes 3145728 | tf_op jit(solution)/shard_map/reduce_prod | solution.py:86
  195.3 2.1 %reshape.134 = f32[24,16,512]{2,1,0:T(8,128)} reshape(f32[24,16,16,32]{3,2,1,0:T(8,128)S(1)} %convert_reduce_fusion) | data formatting | bytes 1572864 | tf_op jit(solution)/shard_map/reshape | solution.py:89
  197.4 2.4 %mul.77 = f32[24,16,512]{2,1,0:T(8,128)} multiply(f32[24,16,512]{2,1,0:T(8,128)} %param.5, f32[24,16,512]{2,1,0:T(8,128)} %reshape.134) | non-fusion elementwise | flops 196608 | bytes 2359296 | tf_op jit(solution)/shard_map/mul | solution.py:89
  (22 shorter events, 0.1 us)
Async XLA Ops:
  0.0 6.8 %copy-start.3 = (f32[6,3]{0,1:T(4,128)S(1)}, f32[6,3]{0,1:T(4,128)}, u32[]{:S(2)}) copy-start(f32[6,3]{0,1:T(4,128)} %param.8) | copy-start | bytes 220
  0.0 6.9 %copy-start.4 = (s32[6,3]{0,1:T(4,128)S(1)}, s32[6,3]{0,1:T(4,128)}, u32[]{:S(2)}) copy-start(s32[6,3]{0,1:T(4,128)} %param.9) | copy-start | bytes 220
  0.0 11.7 %copy-start.2 = (s32[24,6]{0,1:T(8,128)S(1)}, s32[24,6]{0,1:T(8,128)}, u32[]{:S(2)}) copy-start(s32[24,6]{0,1:T(8,128)} %param.7) | copy-start | bytes 1732
  0.0 12.9 %copy-start = (f32[24,16,512]{2,1,0:T(8,128)S(1)}, f32[24,16,512]{2,1,0:T(8,128)}, u32[]{:S(2)}) copy-start(f32[24,16,512]{2,1,0:T(8,128)} %param.5) | copy-start | bytes 2359300
  0.0 110.4 %all-to-all-start = ((bf16[16,18,16,512]{3,2,1,0:T(8,128)(2,1)}), bf16[16,18,16,512]{3,2,1,0:T(8,128)(2,1)}, u32[]{:S(2)}, u32[]{:S(2)}) async-start(bf16[16,18,16,512]{3,2,1,0:T(8,128)(2,1)} %bitcast.67), calls=%async_computation | async-start | bytes 9437184 | tf_op jit(solution)/shard_map/all_to_all | solution.py:83
  131.8 13.7 %copy-start.1 = (bf16[144,16,16,1]{1,2,3,0:T(8,128)(2,1)S(1)}, bf16[144,16,16,1]{1,2,3,0:T(8,128)(2,1)}, u32[]{:S(2)}) copy-start(bf16[144,16,16,1]{1,2,3,0:T(8,128)(2,1)} %copy.42) | copy-start | bytes 221188
where the time goes:
time: 201 us; the launch traced here: 200 us
  matrix products  99.3 us (49%)
  local copies, waits for them, and re-layouts  66.3 us (33%)
  waiting for transfers between devices  16.9 us (8%)
  other arithmetic  10.5 us (5%)
  starting transfers between devices  6.7 us (3%)
    dot_general x1, matrix products, correction_items(): jnp.einsum('szkx,syk->szyx', section, y_matrix, preferred_element_type=jn...  49.1 us
    dot_general x1, matrix products, correction_items(): jnp.einsum('skyx,skz->szyx', quotient, z_matrix, preferred_element_type=j...  32.8 us
    reshape x1, local copies, waits for them, and re-layouts, per_device(): gathered = arrived.reshape((tile_count * slot_count,) + block_shape)[target]  21.4 us
    convert_element_type x1, local copies, waits for them, and re-layouts, correction_items(): section = jnp.einsum('szyk,sxk->szyx', estimates, x_matrix, preferred_ele...  21.1 us
    all_to_all x1, waiting for transfers between devices, per_device(): lax.all_to_all(observed[0], 'tiles', split_axis=0, concat_axis=0, tiled=T...  16.9 us
    gather x1, local copies, waits for them, and re-layouts, per_device(): gathered = arrived.reshape((tile_count * slot_count,) + block_shape)[target]  13.7 us
    dot_general x1, matrix products, correction_items(): jnp.einsum('szyk,skx->szyx', section, x_matrix, preferred_element_type=jn...  10.9 us
    all_to_all x1, starting transfers between devices, per_device(): lax.all_to_all(observed[0], 'tiles', split_axis=0, concat_axis=0, tiled=T...  6.7 us
  transfers between devices with their start and end apart: 1, of which 1 were waited for; matrix products, arithmetic and copies ran while one was open for 43% of the time, Pallas kernels for 0%

commit v1 on v0

v1 whole, which is shorter than its diff:
```python
import functools

import jax
import jax.numpy as jnp
from jax import lax
from jax.experimental import pallas as pl
from jax.experimental.pallas import tpu as pltpu
from jax.sharding import PartitionSpec as P

BX = 32
BY = 16
TAP_REACH = 15
GROUP = 8
VMEM_LIMIT = 56 << 20


def _table(sigma, offset, n, transposed):
    i = lax.broadcasted_iota(jnp.int32, (n, n), 1 if transposed else 0)
    k = lax.broadcasted_iota(jnp.int32, (n, n), 0 if transposed else 1)
    half = n // 2
    d = ((k - i - offset + half) & (n - 1)) - half
    df = d.astype(jnp.float32)
    w = jnp.where(jnp.abs(d) <= TAP_REACH, jnp.exp(-df * df / (2.0 * sigma * sigma)), 0.0)
    return (w / jnp.sum(w, axis=0 if transposed else 1, keepdims=True)).astype(jnp.bfloat16)


def _expand(table, size, position):
    n = table.shape[0]
    tall = position(lax.broadcasted_iota(jnp.int32, (size, n), 0)) == lax.broadcasted_iota(jnp.int32, (size, n), 1)
    wide = position(lax.broadcasted_iota(jnp.int32, (n, size), 1)) == lax.broadcasted_iota(jnp.int32, (n, size), 0)
    rows = jnp.dot(tall.astype(jnp.bfloat16), table, preferred_element_type=jnp.float32).astype(jnp.bfloat16)
    return jnp.dot(rows, wide.astype(jnp.bfloat16), preferred_element_type=jnp.float32)


def _matrices_kernel(sigma, offset, wf, wb, zf, zb):
    v = pl.program_id(0)
    depth = zf.shape[-1] // GROUP
    for transposed, w_out, z_out in ((True, wf, zb), (False, wb, zf)):
        z_table = _table(sigma[v, 0], offset[v, 0], depth, transposed)
        y_table = _table(sigma[v, 1], offset[v, 1], BY, transposed)
        x_table = _table(sigma[v, 2], offset[v, 2], BX, transposed)
        plane = BY * BX
        w_out[0] = (
            _expand(y_table, plane, lambda r: r // BX) * _expand(x_table, plane, lambda r: r % BX)
        ).astype(jnp.bfloat16)
        size = GROUP * depth
        r = lax.broadcasted_iota(jnp.int32, (size, size), 0) // depth
        c = lax.broadcasted_iota(jnp.int32, (size, size), 1) // depth
        full = _expand(z_table, size, lambda q: q % depth)
        z_out[0] = jnp.where(r == c, full, 0.0).astype(jnp.bfloat16)


def _matrices(sigma, offset, depth, plane):
    views = sigma.shape[0]
    size = GROUP * depth
    smem = pl.BlockSpec(memory_space=pltpu.SMEM)
    return pl.pallas_call(
        _matrices_kernel,
        grid=(views,),
        in_specs=[smem, smem],
        out_specs=[
            pl.BlockSpec((1, plane, plane), lambda v: (v, 0, 0)),
            pl.BlockSpec((1, plane, plane), lambda v: (v, 0, 0)),
            pl.BlockSpec((1, size, size), lambda v: (v, 0, 0)),
            pl.BlockSpec((1, size, size), lambda v: (v, 0, 0)),
        ],
        out_shape=[
            jax.ShapeDtypeStruct((views, plane, plane), jnp.bfloat16),
            jax.ShapeDtypeStruct((views, plane, plane), jnp.bfloat16),
            jax.ShapeDtypeStruct((views, size, size), jnp.bfloat16),
            jax.ShapeDtypeStruct((views, size, size), jnp.bfloat16),
        ],
        compiler_params=pltpu.CompilerParams(vmem_limit_bytes=VMEM_LIMIT),
        name="matrices",
    )(sigma, offset)


def _forward_kernel(est, wf, zf, rb):
    size = zf.shape[-1]
    p2 = jnp.dot(est[...], wf[0], preferred_element_type=jnp.float32).astype(jnp.bfloat16)
    for g in range(est.shape[0] // size):
        rows = slice(g * size, (g + 1) * size)
        rb[0, rows] = 1.0 / jnp.dot(zf[0], p2[rows], preferred_element_type=jnp.float32)


def _forward(est, wf, zf):
    views, plane, _ = wf.shape
    rows, size = est.shape[0], zf.shape[-1]
    return pl.pallas_call(
        _forward_kernel,
        grid=(views,),
        in_specs=[
            pl.BlockSpec((rows, plane), lambda v: (0, 0)),
            pl.BlockSpec((1, plane, plane), lambda v: (v, 0, 0)),
            pl.BlockSpec((1, size, size), lambda v: (v, 0, 0)),
        ],
        out_specs=pl.BlockSpec((1, rows, plane), lambda v: (v, 0, 0)),
        out_shape=jax.ShapeDtypeStruct((views, rows, plane), jnp.float32),
        compiler_params=pltpu.CompilerParams(vmem_limit_bytes=VMEM_LIMIT),
        name="forward",
    )(est, wf, zf)


def _backward_kernel(final, slots, obs, rb, wb, zb, *rest):
    if final:
        est, other, out, acc, q1 = rest
    else:
        out, acc, q1 = rest
    v = pl.program_id(0)
    size = zb.shape[-1]
    depth = obs.shape[1]
    blocks = acc.shape[0] // depth
    for g in range(blocks // GROUP):
        rows = slice(g * size, (g + 1) * size)
        picked = jnp.concatenate(
            [obs[jnp.maximum(slots[v, g * GROUP + j], 0)] for j in range(GROUP)], axis=0
        )
        q = (picked.astype(jnp.float32) * rb[0, rows]).astype(jnp.bfloat16)
        q1[rows] = jnp.dot(zb[0], q, preferred_element_type=jnp.float32).astype(jnp.bfloat16)
    correction = jnp.dot(q1[...], wb[0], preferred_element_type=jnp.float32)

    @pl.when(v == 0)
    def _():
        if final:
            acc[...] = est[...] * other[...].astype(jnp.float32)
        else:
            acc[...] = jnp.ones_like(acc)

    for b in range(blocks):
        rows = slice(b * depth, (b + 1) * depth)
        acc[rows] = acc[rows] * jnp.where(slots[v, b] >= 0, correction[rows], 1.0)

    @pl.when(v == pl.num_programs(0) - 1)
    def _():
        out[...] = acc[...].astype(out.dtype)


def _backward(slots, obs, rb, wb, zb, final=None):
    views, rows, plane = rb.shape
    size, depth = zb.shape[-1], obs.shape[1]
    whole = pl.BlockSpec((rows, plane), lambda v, s: (0, 0))
    return pl.pallas_call(
        functools.partial(_backward_kernel, final is not None),
        grid_spec=pltpu.PrefetchScalarGridSpec(
            num_scalar_prefetch=1,
            grid=(views,),
            in_specs=[
                pl.BlockSpec(obs.shape, lambda v, s: (0, 0, 0)),
                pl.BlockSpec((1, rows, plane), lambda v, s: (v, 0, 0)),
                pl.BlockSpec((1, plane, plane), lambda v, s: (v, 0, 0)),
                pl.BlockSpec((1, size, size), lambda v, s: (v, 0, 0)),
            ]
            + ([whole, whole] if final else []),
            out_specs=whole,
            scratch_shapes=[
                pltpu.VMEM((rows, plane), jnp.float32),
                pltpu.VMEM((rows, plane), jnp.bfloat16),
            ],
        ),
        out_shape=jax.ShapeDtypeStruct((rows, plane), jnp.float32 if final else jnp.bfloat16),
        compiler_params=pltpu.CompilerParams(vmem_limit_bytes=VMEM_LIMIT),
        name="backward_own" if final else "backward_other",
    )(slots, obs, rb, wb, zb, *(final or ()))


def _slots(item_tile, first, count, slot_count):
    blocks, views = item_tile.shape
    flat = item_tile.reshape(-1)
    order = jnp.arange(blocks * views, dtype=jnp.int32)
    before = (flat[:, None] == flat[None, :]) & (order[None, :] < order[:, None])
    rank = jnp.sum(before.astype(jnp.int32), axis=1)
    tile = flat - first
    slot = jnp.where((tile >= 0) & (tile < count), tile * slot_count + rank, -1)
    return slot.reshape(blocks, views).T


def per_device(estimate, observed, item_tile, psf_sigma, view_offsets):
    blocks, depth, plane = estimate.shape
    tiles, slot_count = observed.shape[1:3]
    half = tiles // 2
    mine = lax.axis_index("tiles") // half
    groups = [list(range(half)), list(range(half, tiles))]
    swap = [(t, (t + half) % tiles) for t in range(tiles)]

    by_half = observed[0].reshape(2, half, slot_count, depth, plane)

    def exchange(which):
        sent = lax.dynamic_index_in_dim(by_half, which, 0, keepdims=False)
        got = lax.all_to_all(sent, "tiles", 0, 0, axis_index_groups=groups, tiled=True)
        return got.reshape(half * slot_count, depth, plane)

    est = estimate.reshape(blocks * depth, plane)
    est_bf = est.astype(jnp.bfloat16)
    obs_other = exchange(1 - mine)
    est_other = lax.ppermute(est_bf, "tiles", swap)
    item_tile_other = lax.ppermute(item_tile, "tiles", swap)
    obs_own = exchange(mine)

    wf, wb, zf, zb = _matrices(psf_sigma, view_offsets, depth, plane)
    rb_own = _forward(est_bf, wf, zf)
    rb_other = _forward(est_other, wf, zf)
    slots_own = _slots(item_tile, mine * half, half, slot_count)
    slots_other = _slots(item_tile_other, mine * half, half, slot_count)
    sent_back = _backward(slots_other, obs_other, rb_other, wb, zb)
    product = lax.ppermute(sent_back, "tiles", swap)
    updated = _backward(slots_own, obs_own, rb_own, wb, zb, (est, product))
    return updated.reshape(blocks, depth, plane)


def solution(mesh):
    return jax.shard_map(
        per_device,
        mesh=mesh,
        in_specs=(
            P(("groups", "tiles"), None, None),
            P(("groups", "tiles"), None, None, None, None),
            P(("groups", "tiles"), None),
            P(),
            P(),
        ),
        out_specs=P(("groups", "tiles"), None, None),
        check_vma=False,
    )
```

time: 201 us -> 127 us (0.63)
  the two profiles are of different devices: /device:TPU:15 before, /device:TPU:0 now
where the time goes in v1:
time: 127 us; the launch traced here: 126 us
  Pallas kernels  42.7 us (34%)
  blocking collectives  34 us (27%)
  waiting for transfers between devices  29.8 us (23%)
  starting transfers between devices  10.2 us (8%)
  local copies, waits for them, and re-layouts  8.03 us (6%)
  other arithmetic  1.65 us (1%)
    all_to_all x1, blocking collectives, exchange(): lax.all_to_all(sent, 'tiles', 0, 0, axis_index_groups=groups, tiled=True)  34 us
    ppermute x1, waiting for transfers between devices, per_device(): item_tile_other = lax.ppermute(item_tile, 'tiles', swap)  20.4 us
    pallas_call x2, Pallas kernels, _backward(): pl.pallas_call(functools.partial(_backward_kernel, final is not None), gr...  18.3 us
    pallas_call x2, Pallas kernels, _forward(): pl.pallas_call(_forward_kernel, grid=(views,), in_specs=[pl.BlockSpec((ro...  14.4 us
    pallas_call x1, Pallas kernels, _matrices(): pl.pallas_call(_matrices_kernel, grid=(views,), in_specs=[smem, smem], ou...  10 us
    ppermute x1, waiting for transfers between devices, per_device(): product = lax.ppermute(sent_back, 'tiles', swap)  9.4 us
    squeeze x1, local copies, waits for them, and re-layouts, exchange(): sent = lax.dynamic_index_in_dim(by_half, which, 0, keepdims=False)  4.41 us
    all_to_all x1, starting transfers between devices, exchange(): lax.all_to_all(sent, 'tiles', 0, 0, axis_index_groups=groups, tiled=True)  3.76 us
  transfers between devices with their start and end apart: 4, of which 2 were waited for; matrix products, arithmetic and copies ran while one was open for 3% of the time, Pallas kernels for 26%

profile of v1, /device:TPU:0, one launch (start us, length us, event | category | flops | bytes accessed | tf_op | source)
XLA Modules:
  0.0 126.4 jit_solution(10835933852377632833)
XLA Ops:
  0.0 4.4 %dynamic-slice_bitcast_fusion = (bf16[8,18,16,512]{3,2,1,0:T(8,128)(2,1)S(1)}, bf16[8,18,16,512]{3,2,1,0:T(8,128)(2,1)}) fusion(bf16[2,8,18,16,512]{4,3,2,1,0:T(8,128)(2,1)} %bitcast.16, s32[]{:T(128)S(6)} %select_n.25, s32[]{:T(128)S(6)} %select_n.23), kind=kLoop, calls=%fused_computation | loop fusion | bytes 9437192 | tf_op jit(solution)/shard_map/jit(dynamic_index_in_dim)/squeeze | solution.py:188
  4.4 34.0 %all_to_all.10 = bf16[8,18,16,512]{3,2,1,0:T(8,128)(2,1)} all-to-all(bf16[8,18,16,512]{3,2,1,0:T(8,128)(2,1)S(1)} %get-tuple-element.13), channel_id=1, replica_groups={{0,1,2,3,4,5,6,7},{8,9,10,11,12,13,14,15},{16,17,18,19,20,21,22,23},{24..., dimensions={0} | all-to-all | bytes 4718592 | tf_op jit(solution)/shard_map/all_to_all | solution.py:189
  38.4 3.8 %all-to-all-start = ((bf16[8,18,16,512]{3,2,1,0:T(8,128)(2,1)}), bf16[8,18,16,512]{3,2,1,0:T(8,128)(2,1)S(1)}, u32[]{:S(2)}, u32[]{:S(2)}) async-start(bf16[8,18,16,512]{3,2,1,0:T(8,128)(2,1)} %get-tuple-element.14), calls=%async_computation | async-start | bytes 4718592 | tf_op jit(solution)/shard_map/all_to_all | solution.py:189
  42.3 0.0 copy-start.2
  42.3 2.7 %collective-permute-start.1 = (bf16[384,512]{1,0:T(8,128)(2,1)S(1)}, bf16[384,512]{1,0:T(8,128)(2,1)S(1)}, u32[]{:S(2)}, u32[]{:S(2)}) collective-permute-start(bf16[384,512]{1,0:T(8,128)(2,1)S(1)} %bitcast_convert_fusion.est), channel_id=1, source_target_pairs={{0,8},{1,9},{2,10},{3,11},{4,12},{5,13},{6,14},{7,15},{8,0},{9,1},... | collective-permute-start | bytes 1179656 | tf_op jit(solution)/shard_map/ppermute | solution.py:195
  45.0 0.3 collective-permute-start
  45.3 0.7 copy.16.sigma
  46.0 0.7 copy.17.offset
  46.7 10.0 %matrices.1 = (bf16[6,512,512]{2,1,0:T(8,128)(2,1)}, bf16[6,512,512]{2,1,0:T(8,128)(2,1)}, bf16[6,128,128]{2,1,0:T(8,128)(2,1)}, bf16[6,128,128]{2,1,0:T(8,128)(2,1)}) custom-call(f32[6,3]{1,0:T(8,128)} %copy.16.sigma, s32[6,3]{1,0:T(8,128)} %copy.17.offset), custom_call_target="tpu_custom_call" | custom-call | tf_op jit(solution)/shard_map/matrices/pallas_call | solution.py:57
  56.7 20.4 %collective-permute-done = s32[24,6]{0,1:T(8,128)S(1)} collective-permute-done((s32[24,6]{0,1:T(8,128)S(1)}, s32[24,6]{0,1:T(8,128)S(1)}, u32[]{:S(2)}, u32[]{:S(2)}) %collective-permute-start) | collective-permute-done | bytes 608 | tf_op jit(solution)/shard_map/ppermute | solution.py:196
  77.0 0.1 copy.18
  77.1 0.1 eq.34
  77.2 0.2 convert_reduce_fusion
  77.4 0.1 reduce_sum.25
  77.5 0.1 copy.19
  77.6 0.6 select_bitcast_fusion.slots
  78.2 0.0 collective-permute-done.1.est
  78.2 0.7 copy-done.3
  79.0 7.2 %forward.3.rb = f32[6,384,512]{2,1,0:T(8,128)} custom-call(bf16[384,512]{1,0:T(8,128)(2,1)} %copy-done.3, bf16[6,512,512]{2,1,0:T(8,128)(2,1)} %get-tuple-element.9.wf, bf16[6,128,128]{2,1,0:T(8,128)(2,1)} %get-tuple-element.10.zf), custom_call_target="tpu_custom_call" | custom-call | tf_op jit(solution)/shard_map/forward/pallas_call | solution.py:89
  86.2 8.9 %backward_other.1 = bf16[384,512]{1,0:T(8,128)(2,1)} custom-call(s32[6,24]{1,0:T(8,128)} %select_bitcast_fusion.slots, bf16[144,16,512]{2,1,0:T(8,128)(2,1)} %bitcast.14, f32[6,384,512]{2,1,0:T(8,128)} %forward.3.rb, bf16[6,512,512]{2,1,0:T(8,128)(2,1)} %get-tuple-element.11.wb, bf16[6,128,128]{2,1,0:T(8,128)(2,1)} %get-tuple-element.12.zb), custom_call_target="tpu_custom_call" | custom-call | tf_op jit(solution)/shard_map/backward_other/pallas_call | solution.py:142
  95.1 3.4 %collective-permute-start.2 = (bf16[384,512]{1,0:T(8,128)(2,1)}, bf16[384,512]{1,0:T(8,128)(2,1)S(1)}, u32[]{:S(2)}, u32[]{:S(2)}) collective-permute-start(bf16[384,512]{1,0:T(8,128)(2,1)} %backward_other.1), channel_id=1, source_target_pairs={{0,8},{1,9},{2,10},{3,11},{4,12},{5,13},{6,14},{7,15},{8,0},{9,1},... | collective-permute-start | bytes 1179656 | tf_op jit(solution)/shard_map/ppermute | solution.py:205
  98.5 0.1 copy.14
  98.6 7.2 %forward.2.rb = f32[6,384,512]{2,1,0:T(8,128)} custom-call(bf16[384,512]{1,0:T(8,128)(2,1)} %copy-done.2, bf16[6,512,512]{2,1,0:T(8,128)(2,1)} %get-tuple-element.9.wf, bf16[6,128,128]{2,1,0:T(8,128)(2,1)} %get-tuple-element.10.zf), custom_call_target="tpu_custom_call" | custom-call | tf_op jit(solution)/shard_map/forward/pallas_call | solution.py:89
  105.8 0.1 eq.30
  105.9 0.2 convert_reduce_fusion.1
  106.1 0.1 reduce_sum.23
  106.2 0.1 copy.15
  106.3 0.6 select_bitcast_fusion.1.slots
  106.9 0.0 all-to-all-done
  106.9 9.4 %collective-permute-done.2.rest_1_ = bf16[384,512]{1,0:T(8,128)(2,1)S(1)} collective-permute-done((bf16[384,512]{1,0:T(8,128)(2,1)}, bf16[384,512]{1,0:T(8,128)(2,1)S(1)}, u32[]{:S(2)}, u32[]{:S(2)}) %collective-permute-start.2) | collective-permute-done | bytes 393248 | tf_op jit(solution)/shard_map/ppermute | solution.py:205
  116.3 0.8 copy-done.4
  117.1 9.4 %backward_own.1 = f32[384,512]{1,0:T(8,128)} custom-call(s32[6,24]{1,0:T(8,128)} %select_bitcast_fusion.1.slots, bf16[144,16,512]{2,1,0:T(8,128)(2,1)} %bitcast.15, f32[6,384,512]{2,1,0:T(8,128)} %forward.2.rb, bf16[6,512,512]{2,1,0:T(8,128)(2,1)} %get-tuple-element.11.wb, bf16[6,128,128]{2,1,0:T(8,128)(2,1)} %get-tuple-element.12.zb, f32[384,512]{1,0:T(8,128)} %bitcast.17, ...), custom_call_target="tpu_custom_call" | custom-call | tf_op jit(solution)/shard_map/backward_own/pallas_call | solution.py:142
  (14 shorter events, 0.1 us)
Async XLA Ops:
  38.4 3.8 %copy-start.1 = (f32[24,16,512]{2,1,0:T(8,128)S(1)}, f32[24,16,512]{2,1,0:T(8,128)}, u32[]{:S(2)}) copy-start(f32[24,16,512]{2,1,0:T(8,128)} %param.5) | copy-start | bytes 2359300
  38.4 6.5 %copy-start.5 = (s32[24,6]{0,1:T(8,128)S(1)}, s32[24,6]{0,1:T(8,128)}, u32[]{:S(2)}) copy-start(s32[24,6]{0,1:T(8,128)} %param.7) | copy-start | bytes 1732
  38.4 6.9 %copy-start.6 = (f32[6,3]{0,1:T(4,128)S(1)}, f32[6,3]{0,1:T(4,128)}, u32[]{:S(2)}) copy-start(f32[6,3]{0,1:T(4,128)} %param.8) | copy-start | bytes 220
  38.4 7.5 %copy-start.7 = (s32[6,3]{0,1:T(4,128)S(1)}, s32[6,3]{0,1:T(4,128)}, u32[]{:S(2)}) copy-start(s32[6,3]{0,1:T(4,128)} %param.9) | copy-start | bytes 220
  38.4 68.5 %all-to-all-start = ((bf16[8,18,16,512]{3,2,1,0:T(8,128)(2,1)}), bf16[8,18,16,512]{3,2,1,0:T(8,128)(2,1)S(1)}, u32[]{:S(2)}, u32[]{:S(2)}) async-start(bf16[8,18,16,512]{3,2,1,0:T(8,128)(2,1)} %get-tuple-element.14), calls=%async_computation | async-start | bytes 4718592 | tf_op jit(solution)/shard_map/all_to_all | solution.py:189
  42.3 43.9 %copy-start.2 = (bf16[384,512]{1,0:T(8,128)(2,1)}, bf16[384,512]{1,0:T(8,128)(2,1)S(1)}, u32[]{:S(2)}) copy-start(bf16[384,512]{1,0:T(8,128)(2,1)S(1)} %bitcast_convert_fusion.est) | copy-start | bytes 1179652
  42.3 36.0 %collective-permute-start.1 = (bf16[384,512]{1,0:T(8,128)(2,1)S(1)}, bf16[384,512]{1,0:T(8,128)(2,1)S(1)}, u32[]{:S(2)}, u32[]{:S(2)}) collective-permute-start(bf16[384,512]{1,0:T(8,128)(2,1)S(1)} %bitcast_convert_fusion.est), channel_id=1, source_target_pairs={{0,8},{1,9},{2,10},{3,11},{4,12},{5,13},{6,14},{7,15},{8,0},{9,1},... | collective-permute-start | bytes 1179656 | tf_op jit(solution)/shard_map/ppermute | solution.py:195
  45.0 32.1 %collective-permute-start = (s32[24,6]{0,1:T(8,128)S(1)}, s32[24,6]{0,1:T(8,128)S(1)}, u32[]{:S(2)}, u32[]{:S(2)}) collective-permute-start(s32[24,6]{0,1:T(8,128)S(1)} %copy-done.5), channel_id=1, source_target_pairs={{0,8},{1,9},{2,10},{3,11},{4,12},{5,13},{6,14},{7,15},{8,0},{9,1},... | collective-permute-start | bytes 1736 | tf_op jit(solution)/shard_map/ppermute | solution.py:196
  78.2 0.7 copy-start.3
  95.1 21.2 %collective-permute-start.2 = (bf16[384,512]{1,0:T(8,128)(2,1)}, bf16[384,512]{1,0:T(8,128)(2,1)S(1)}, u32[]{:S(2)}, u32[]{:S(2)}) collective-permute-start(bf16[384,512]{1,0:T(8,128)(2,1)} %backward_other.1), channel_id=1, source_target_pairs={{0,8},{1,9},{2,10},{3,11},{4,12},{5,13},{6,14},{7,15},{8,0},{9,1},... | collective-permute-start | bytes 1179656 | tf_op jit(solution)/shard_map/ppermute | solution.py:205
  106.9 9.4 %copy-start = (bf16[8,18,16,512]{3,2,1,0:T(8,128)(2,1)}, bf16[8,18,16,512]{3,2,1,0:T(8,128)(2,1)S(1)}, u32[]{:S(2)}) copy-start(bf16[8,18,16,512]{3,2,1,0:T(8,128)(2,1)S(1)} %all-to-all-done) | copy-start | bytes 7077892
  116.3 0.8 copy-start.4

commit v2 on v1

--- a/solution.py
+++ b/solution.py
@@ -11,7 +11,7 @@
 BY = 16
 TAP_REACH = 15
 GROUP = 8
-VMEM_LIMIT = 56 << 20
+VMEM_LIMIT = 28 << 20
 
 
 def _table(sigma, offset, n, transposed):
@@ -65,8 +65,8 @@
             pl.BlockSpec((1, size, size), lambda v: (v, 0, 0)),
         ],
         out_shape=[
-            jax.ShapeDtypeStruct((views, plane, plane), jnp.bfloat16),
-            jax.ShapeDtypeStruct((views, plane, plane), jnp.bfloat16),
+            pltpu.HBM((views, plane, plane), jnp.bfloat16),
+            pltpu.HBM((views, plane, plane), jnp.bfloat16),
             jax.ShapeDtypeStruct((views, size, size), jnp.bfloat16),
             jax.ShapeDtypeStruct((views, size, size), jnp.bfloat16),
         ],
@@ -95,72 +95,145 @@
             pl.BlockSpec((1, size, size), lambda v: (v, 0, 0)),
         ],
         out_specs=pl.BlockSpec((1, rows, plane), lambda v: (v, 0, 0)),
-        out_shape=jax.ShapeDtypeStruct((views, rows, plane), jnp.float32),
+        out_shape=pltpu.HBM((views, rows, plane), jnp.float32),
         compiler_params=pltpu.CompilerParams(vmem_limit_bytes=VMEM_LIMIT),
         name="forward",
     )(est, wf, zf)
 
 
-def _backward_kernel(final, slots, obs, rb, wb, zb, *rest):
-    if final:
-        est, other, out, acc, q1 = rest
-    else:
-        out, acc, q1 = rest
-    v = pl.program_id(0)
-    size = zb.shape[-1]
-    depth = obs.shape[1]
-    blocks = acc.shape[0] // depth
-    for g in range(blocks // GROUP):
-        rows = slice(g * size, (g + 1) * size)
-        picked = jnp.concatenate(
-            [obs[jnp.maximum(slots[v, g * GROUP + j], 0)] for j in range(GROUP)], axis=0
-        )
-        q = (picked.astype(jnp.float32) * rb[0, rows]).astype(jnp.bfloat16)
-        q1[rows] = jnp.dot(zb[0], q, preferred_element_type=jnp.float32).astype(jnp.bfloat16)
-    correction = jnp.dot(q1[...], wb[0], preferred_element_type=jnp.float32)
-
-    @pl.when(v == 0)
-    def _():
-        if final:
-            acc[...] = est[...] * other[...].astype(jnp.float32)
-        else:
-            acc[...] = jnp.ones_like(acc)
-
-    for b in range(blocks):
-        rows = slice(b * depth, (b + 1) * depth)
-        acc[rows] = acc[rows] * jnp.where(slots[v, b] >= 0, correction[rows], 1.0)
-
-    @pl.when(v == pl.num_programs(0) - 1)
-    def _():
-        out[...] = acc[...].astype(out.dtype)
-
-
-def _backward(slots, obs, rb, wb, zb, final=None):
-    views, rows, plane = rb.shape
-    size, depth = zb.shape[-1], obs.shape[1]
-    whole = pl.BlockSpec((rows, plane), lambda v, s: (0, 0))
+def _fetch(pairs, sems):
+    copies = [pltpu.make_async_copy(src, dst, sems.at[n]) for n, (src, dst) in enumerate(pairs)]
+    for copy in copies:
+        copy.start()
+    return copies
+
+
+def _spans(total, size):
+    return [slice(first, first + size) for first in range(0, total, size)]
+
+
+def _quotient(slots, obs, v, g):
+    return jnp.concatenate([obs[jnp.maximum(slots[v, g * GROUP + j], 0)] for j in range(GROUP)], axis=0)
+
+
+def _multiply_in(slots, v, acc, correction, depth):
+    for b, span in enumerate(_spans(acc.shape[0], depth)):
+        acc[span] = acc[span] * jnp.where(slots[v, b] >= 0, correction[span], 1.0)
+
+
+def _places(arrays, buffer, piece=18):
+    out, first = [], 0
+    for array in arrays:
+        for span in _spans(array.shape[0], piece):
+            length = min(span.stop, array.shape[0]) - span.start
+            out.append((array.at[pl.ds(span.start, length)], buffer.at[pl.ds(first + span.start, length)]))
+        first += array.shape[0]
+    return out
+
+
+def _backward_views(slots, obs, rb, wb, zb, q1, acc, arrive_rb, arrive_wb, finish):
+    views, rows, size, depth = rb.shape[0], rb.shape[1], zb.shape[-1], obs.shape[1]
+    for v in range(views + 1):
+        if v < views:
+            arrive_rb(v)
+        if v > 0:
+            arrive_wb(v - 1)
+        if v == views:
+            finish()
+        if v < views:
+            for g, span in enumerate(_spans(rows, size)):
+                q = (_quotient(slots, obs, v, g).astype(jnp.float32) * rb[v, span]).astype(jnp.bfloat16)
+                q1[v, span] = jnp.dot(zb[v], q, preferred_element_type=jnp.float32).astype(jnp.bfloat16)
+        if v > 0:
+            correction = jnp.dot(q1[v - 1], wb[v - 1], preferred_element_type=jnp.float32)
+            _multiply_in(slots, v - 1, acc, correction, depth)
+
+
+def _other_kernel(n_obs, n_prior, slots, est, zf, zb, *rest):
+    prior, rest = rest[:n_prior], rest[n_prior:]
+    wf_hbm, wb_hbm = rest[:2]
+    obs_hbm, rest = rest[2 : 2 + n_obs], rest[2 + n_obs :]
+    out, wf, wb, obs, p2, rb, acc, sems = rest
+    views, size = wf.shape[0], zf.shape[-1]
+    pairs = [(wf_hbm.at[v], wf.at[v]) for v in range(views)] + _places(obs_hbm, obs)
+    last = len(pairs)
+    pairs += [(wb_hbm.at[v], wb.at[v]) for v in range(views)]
+    copies = _fetch(pairs, sems)
+    acc[...] = prior[0][...].astype(jnp.float32) if n_prior else jnp.ones_like(acc)
+    for v in range(views + 1):
+        if v < views:
+            copies[v].wait()
+            p2[v] = jnp.dot(est[...], wf[v], preferred_element_type=jnp.float32).astype(jnp.bfloat16)
+        if v > 0:
+            for span in _spans(rb.shape[1], size):
+                rb[v - 1, span] = 1.0 / jnp.dot(zf[v - 1], p2[v - 1, span], preferred_element_type=jnp.float32)
+    for copy in copies[views:]:
+        copy.wait()
+    nothing = lambda *_: None
+    _backward_views(slots, obs, rb, wb, zb, p2, acc, nothing, nothing, nothing)
+    out[...] = acc[...].astype(out.dtype)
+
+
+def _own_kernel(n_prior, slots, zb, obs, *rest):
+    prior, rest = rest[:n_prior], rest[n_prior:]
+    rb_hbm, wb_hbm, est_hbm, acc, rb, wb, est, q1, sems = rest
+    views = wb.shape[0]
+    pairs = []
+    for v in range(views):
+        pairs += [(rb_hbm.at[v], rb.at[v]), (wb_hbm.at[v], wb.at[v])]
+    copies = _fetch(pairs + [(est_hbm, est)], sems)
+    acc[...] = jnp.ones_like(acc)
+
+    def finish():
+        copies[-1].wait()
+        for factor in (est, *prior):
+            acc[...] = acc[...] * factor[...].astype(jnp.float32)
+
+    _backward_views(
+        slots, obs, rb, wb, zb, q1, acc, lambda v: copies[2 * v].wait(), lambda v: copies[2 * v + 1].wait(), finish
+    )
+
+
+def _call(kernel, name, out_shape, slots, whole, far, obs, near, scratch):
+    count = sum(o.shape[0] for o in obs)
+    smem, vmem, hbm = (pl.BlockSpec(memory_space=m) for m in (pltpu.SMEM, pltpu.VMEM, pltpu.HBM))
+    fetched = (*far, *obs, *near)
+    n_copies = sum(w.shape[0] for w in far) + sum(len(_spans(o.shape[0], 18)) for o in obs) + len(near)
     return pl.pallas_call(
-        functools.partial(_backward_kernel, final is not None),
-        grid_spec=pltpu.PrefetchScalarGridSpec(
-            num_scalar_prefetch=1,
-            grid=(views,),
-            in_specs=[
-                pl.BlockSpec(obs.shape, lambda v, s: (0, 0, 0)),
-                pl.BlockSpec((1, rows, plane), lambda v, s: (v, 0, 0)),
-                pl.BlockSpec((1, plane, plane), lambda v, s: (v, 0, 0)),
-                pl.BlockSpec((1, size, size), lambda v, s: (v, 0, 0)),
-            ]
-            + ([whole, whole] if final else []),
-            out_specs=whole,
-            scratch_shapes=[
-                pltpu.VMEM((rows, plane), jnp.float32),
-                pltpu.VMEM((rows, plane), jnp.bfloat16),
-            ],
-        ),
-        out_shape=jax.ShapeDtypeStruct((rows, plane), jnp.float32 if final else jnp.bfloat16),
+        kernel,
+        in_specs=[smem] + [vmem] * len(whole) + [hbm] * len(fetched),
+        out_specs=vmem,
+        out_shape=out_shape,
+        scratch_shapes=[pltpu.VMEM(w.shape, w.dtype) for w in far]
+        + [pltpu.VMEM((count, *o.shape[1:]), o.dtype) for o in obs[:1]]
+        + [pltpu.VMEM(w.shape, w.dtype) for w in near]
+        + scratch
+        + [pltpu.SemaphoreType.DMA((n_copies,))],
         compiler_params=pltpu.CompilerParams(vmem_limit_bytes=VMEM_LIMIT),
-        name="backward_own" if final else "backward_other",
-    )(slots, obs, rb, wb, zb, *(final or ()))
+        name=name,
+    )(slots, *whole, *(pltpu.with_memory_space_constraint(x, pltpu.HBM) for x in fetched))
+
+
+def _other(slots, est, obs, matrices, prior=()):
+    wf, wb, zf, zb = matrices
+    rows, plane = est.shape
+    scratch = [
+        pltpu.VMEM((wf.shape[0], rows, plane), jnp.bfloat16),
+        pltpu.VMEM((wf.shape[0], rows, plane), jnp.float32),
+        pltpu.VMEM((rows, plane), jnp.float32),
+    ]
+    kernel = functools.partial(_other_kernel, len(obs), len(prior))
+    out = pltpu.HBM((rows, plane), jnp.bfloat16)
+    return _call(kernel, "other", out, slots, (est, zf, zb, *prior), (wf, wb), obs, (), scratch)
+
+
+def _own(slots, est, obs, rb, matrices, prior):
+    _, wb, _, zb = matrices
+    scratch = [pltpu.VMEM(rb.shape, jnp.bfloat16)]
+    kernel = functools.partial(_own_kernel, len(prior))
+    out = jax.ShapeDtypeStruct(est.shape, jnp.float32)
+    whole = [zb] + [pltpu.with_memory_space_constraint(x, pltpu.VMEM) for x in (obs, *prior)]
+    return _call(kernel, "own", out, slots, whole, (rb, wb), (), (est,), scratch)
 
 
 def _slots(item_tile, first, count, slot_count):
@@ -184,26 +257,27 @@
 
     by_half = observed[0].reshape(2, half, slot_count, depth, plane)
 
-    def exchange(which):
-        sent = lax.dynamic_index_in_dim(by_half, which, 0, keepdims=False)
+    def exchange(sent):
         got = lax.all_to_all(sent, "tiles", 0, 0, axis_index_groups=groups, tiled=True)
         return got.reshape(half * slot_count, depth, plane)
 
     est = estimate.reshape(blocks * depth, plane)
     est_bf = est.astype(jnp.bfloat16)
-    obs_other = exchange(1 - mine)
     est_other = lax.ppermute(est_bf, "tiles", swap)
     item_tile_other = lax.ppermute(item_tile, "tiles", swap)
-    obs_own = exchange(mine)
-
-    wf, wb, zf, zb = _matrices(psf_sigma, view_offsets, depth, plane)
-    rb_own = _forward(est_bf, wf, zf)
-    rb_other = _forward(est_other, wf, zf)
+    obs_other = exchange(lax.dynamic_index_in_dim(by_half, 1 - mine, 0, keepdims=False))
+    matrices = _matrices(psf_sigma, view_offsets, depth, plane)
+    rb_own = _forward(est_bf, matrices[0], matrices[2])
     slots_own = _slots(item_tile, mine * half, half, slot_count)
     slots_other = _slots(item_tile_other, mine * half, half, slot_count)
-    sent_back = _backward(slots_other, obs_other, rb_other, wb, zb)
-    product = lax.ppermute(sent_back, "tiles", swap)
-    updated = _backward(slots_own, obs_own, rb_own, wb, zb, (est, product))
+    by_half_2, _ = lax.optimization_barrier((by_half, matrices[2]))
+    sent = lax.dynamic_index_in_dim(by_half_2, mine, 0, keepdims=False)
+    sent, rb_own, est_other, slots_own, slots_other = lax.optimization_barrier(
+        (sent, rb_own, est_other, slots_own, slots_other)
+    )
+    obs_own = exchange(sent)
+    product = lax.ppermute(_other(slots_other, est_other, [obs_other], matrices), "tiles", swap)
+    updated = _own(slots_own, est, obs_own, rb_own, matrices, [product])
     return updated.reshape(blocks, depth, plane)
 
 

time: 127 us -> 94.3 us (0.74)
  blocking collectives: 34 us -> 0 us
  Pallas kernels: 42.7 us -> 28.7 us
  waiting for transfers between devices: 29.8 us -> 41.1 us
  starting transfers between devices: 10.2 us -> 14.6 us
    all_to_all x1 -> x0, blocking collectives: 34 us -> none  [exchange(): lax.all_to_all(sent, 'tiles', 0, 0, axis_index_groups=groups, tiled=True)]
    all_to_all x1 -> x2, waiting for transfers between devices: 0.01 us -> 30.5 us  [exchange(): lax.all_to_all(sent, 'tiles', 0, 0, axis_index_groups=groups, tiled=True)]
    ppermute x1, waiting for transfers between devices: 20.4 us -> 2.98 us  [per_device(): item_tile_other = lax.ppermute(item_tile, 'tiles', swap)]
    pallas_call x2 -> x1, Pallas kernels: 14.4 us -> 4.9 us  [_forward(): pl.pallas_call(_forward_kernel, grid=(views,), in_specs=[pl.BlockSpec((ro...]
    ppermute x1, waiting for transfers between devices: 9.4 us -> 0.01 us  [per_device(): lax.ppermute(_other(slots_other, est_other, [obs_other], matrices), 'tile...]
    ppermute x1, waiting for transfers between devices: 0.01 us -> 7.65 us  [per_device(): est_other = lax.ppermute(est_bf, 'tiles', swap)]
    all_to_all x1 -> x2, starting transfers between devices: 3.76 us -> 10.7 us  [exchange(): lax.all_to_all(sent, 'tiles', 0, 0, axis_index_groups=groups, tiled=True)]
    pallas_call x2, Pallas kernels: 18.3 us -> 13.9 us  [_call(): pl.pallas_call(kernel, in_specs=[smem] + [vmem] * len(whole) + [hbm] * le...]
  transfers between devices with their start and end apart: 4 -> 5, of which waited for: 2 -> 4; matrix products, arithmetic and copies ran while one was open for 3% -> 5% of each run, Pallas kernels for 26% -> 24%
where the time goes in v2:
time: 94.3 us; the launch traced here: 93.9 us
  waiting for transfers between devices  41.1 us (44%)
  Pallas kernels  28.7 us (30%)
  starting transfers between devices  14.6 us (15%)
  local copies, waits for them, and re-layouts  8.97 us (10%)
    all_to_all x2, waiting for transfers between devices, exchange(): lax.all_to_all(sent, 'tiles', 0, 0, axis_index_groups=groups, tiled=True)  30.5 us
    pallas_call x2, Pallas kernels, _call(): pl.pallas_call(kernel, in_specs=[smem] + [vmem] * len(whole) + [hbm] * le...  13.9 us
    all_to_all x2, starting transfers between devices, exchange(): lax.all_to_all(sent, 'tiles', 0, 0, axis_index_groups=groups, tiled=True)  10.7 us
    pallas_call x1, Pallas kernels, _matrices(): pl.pallas_call(_matrices_kernel, grid=(views,), in_specs=[smem, smem], ou...  9.88 us
    ppermute x1, waiting for transfers between devices, per_device(): est_other = lax.ppermute(est_bf, 'tiles', swap)  7.65 us
    pallas_call x1, Pallas kernels, _forward(): pl.pallas_call(_forward_kernel, grid=(views,), in_specs=[pl.BlockSpec((ro...  4.9 us
    squeeze x1, local copies, waits for them, and re-layouts, per_device(): sent = lax.dynamic_index_in_dim(by_half_2, mine, 0, keepdims=False)  3.44 us
    squeeze x1, local copies, waits for them, and re-layouts, per_device(): lax.dynamic_index_in_dim(by_half, 1 - mine, 0, keepdims=False)  3.25 us
  transfers between devices with their start and end apart: 5, of which 4 were waited for; matrix products, arithmetic and copies ran while one was open for 5% of the time, Pallas kernels for 24%

profile of v2, /device:TPU:0, one launch (start us, length us, event | category | flops | bytes accessed | tf_op | source)
XLA Modules:
  0.0 93.9 jit_solution(16741551375981509093)
XLA Ops:
  0.0 3.2 %dynamic-slice_bitcast_fusion = bf16[8,18,16,512]{3,2,1,0:T(8,128)(2,1)} fusion(bf16[2,8,18,16,512]{4,3,2,1,0:T(8,128)(2,1)} %bitcast.15, s32[]{:T(128)S(6)} %select_n.25), kind=kLoop, calls=%fused_computation | loop fusion | bytes 4718596 | tf_op jit(solution)/shard_map/jit(dynamic_index_in_dim)/squeeze | solution.py:268
  3.3 5.4 %all-to-all-start.1 = ((bf16[8,18,16,512]{3,2,1,0:T(8,128)(2,1)}), bf16[8,18,16,512]{3,2,1,0:T(8,128)(2,1)}, u32[]{:S(2)}, u32[]{:S(2)}) async-start(bf16[8,18,16,512]{3,2,1,0:T(8,128)(2,1)} %dynamic-slice_bitcast_fusion), calls=%async_computation.1 | async-start | bytes 4718592 | tf_op jit(solution)/shard_map/all_to_all | solution.py:261
  8.7 3.2 %collective-permute-start.1 = (s32[24,6]{0,1:T(8,128)S(1)}, s32[24,6]{0,1:T(8,128)S(1)}, u32[]{:S(2)}, u32[]{:S(2)}) collective-permute-start(s32[24,6]{0,1:T(8,128)S(1)} %copy-done.7), channel_id=1, source_target_pairs={{0,8},{1,9},{2,10},{3,11},{4,12},{5,13},{6,14},{7,15},{8,0},{9,1},... | collective-permute-start | bytes 1736 | tf_op jit(solution)/shard_map/ppermute | solution.py:267
  11.9 0.1 collective-permute-start
  12.0 0.1 copy.16
  12.1 0.1 copy.14.sigma
  12.2 0.1 copy.15.offset
  12.3 0.1 eq.30
  12.4 0.2 convert_reduce_fusion.1
  12.6 0.1 reduce_sum.23
  12.7 0.1 copy.17
  12.8 9.9 %matrices.1 = (bf16[6,512,512]{2,1,0:T(8,128)(2,1)}, bf16[6,512,512]{2,1,0:T(8,128)(2,1)}, bf16[6,128,128]{2,1,0:T(8,128)(2,1)S(1)}, bf16[6,128,128]{2,1,0:T(8,128)(2,1)S(1)}) custom-call(f32[6,3]{1,0:T(8,128)S(1)} %copy.14.sigma, s32[6,3]{1,0:T(8,128)S(1)} %copy.15.offset), custom_call_target="tpu_custom_call" | custom-call | tf_op jit(solution)/shard_map/matrices/pallas_call | solution.py:57
  22.7 0.7 copy-done.1
  23.4 0.7 copy-done.3
  24.0 3.4 %dynamic-slice_bitcast_fusion.1 = bf16[8,18,16,512]{3,2,1,0:T(8,128)(2,1)} fusion(bf16[2,8,18,16,512]{4,3,2,1,0:T(8,128)(2,1)} %bitcast.16, s32[]{:T(128)S(6)} %select_n.22), kind=kLoop, calls=%fused_computation.1 | loop fusion | bytes 4718596 | tf_op jit(solution)/shard_map/jit(dynamic_index_in_dim)/squeeze | solution.py:274
  27.5 0.0 copy-done.4
  27.5 4.9 %forward.1.rest_1_ = f32[6,384,512]{2,1,0:T(8,128)} custom-call(bf16[384,512]{1,0:T(8,128)(2,1)S(1)} %bitcast_convert_fusion.est, bf16[6,512,512]{2,1,0:T(8,128)(2,1)S(1)} %copy-done, bf16[6,128,128]{2,1,0:T(8,128)(2,1)S(1)} %copy-done.4), custom_call_target="tpu_custom_call" | custom-call | tf_op jit(solution)/shard_map/forward/pallas_call | solution.py:89
  32.4 3.0 %collective-permute-done.1 = s32[24,6]{0,1:T(8,128)S(1)} collective-permute-done((s32[24,6]{0,1:T(8,128)S(1)}, s32[24,6]{0,1:T(8,128)S(1)}, u32[]{:S(2)}, u32[]{:S(2)}) %collective-permute-start.1) | collective-permute-done | bytes 608 | tf_op jit(solution)/shard_map/ppermute | solution.py:267
  35.4 0.1 copy.18
  35.5 0.1 eq.34
  35.6 0.2 convert_reduce_fusion
  35.8 0.1 reduce_sum.25
  35.9 0.1 copy.19
  36.0 7.7 %collective-permute-done.est = bf16[384,512]{1,0:T(8,128)(2,1)} collective-permute-done((bf16[384,512]{1,0:T(8,128)(2,1)S(1)}, bf16[384,512]{1,0:T(8,128)(2,1)}, u32[]{:S(2)}, u32[]{:S(2)}) %collective-permute-start) | collective-permute-done | bytes 393248 | tf_op jit(solution)/shard_map/ppermute | solution.py:266
  43.6 2.2 %all-to-all-done.1 = bf16[8,18,16,512]{3,2,1,0:T(8,128)(2,1)} async-done(((bf16[8,18,16,512]{3,2,1,0:T(8,128)(2,1)}), bf16[8,18,16,512]{3,2,1,0:T(8,128)(2,1)}, u32[]{:S(2)}, u32[]{:S(2)}) %all-to-all-start.1) | async-done | bytes 2359328 | tf_op jit(solution)/shard_map/all_to_all | solution.py:261
  45.8 5.3 %all-to-all-start = ((bf16[8,18,16,512]{3,2,1,0:T(8,128)(2,1)}), bf16[8,18,16,512]{3,2,1,0:T(8,128)(2,1)S(1)}, u32[]{:S(2)}, u32[]{:S(2)}) async-start(bf16[8,18,16,512]{3,2,1,0:T(8,128)(2,1)} %dynamic-slice_bitcast_fusion.1), calls=%async_computation | async-start | bytes 4718592 | tf_op jit(solution)/shard_map/all_to_all | solution.py:261
  51.0 0.0 copy-done.5
  51.1 7.9 %other.1 = bf16[384,512]{1,0:T(8,128)(2,1)} custom-call(s32[6,24]{1,0:T(8,128)S(1)} %select_bitcast_fusion.slots, bf16[384,512]{1,0:T(8,128)(2,1)} %collective-permute-done.est, bf16[6,128,128]{2,1,0:T(8,128)(2,1)S(1)} %copy-done.5, bf16[6,128,128]{2,1,0:T(8,128)(2,1)S(1)} %copy-done.2, bf16[6,512,512]{2,1,0:T(8,128)(2,1)} %get-tuple-element.17.wf.rest_0_, ...), custom_call_target="tpu_custom_call" | custom-call | tf_op jit(solution)/shard_map/other/pallas_call | solution.py:202
  59.0 0.6 collective-permute-start.2
  59.6 28.3 %all-to-all-done = bf16[8,18,16,512]{3,2,1,0:T(8,128)(2,1)S(1)} async-done(((bf16[8,18,16,512]{3,2,1,0:T(8,128)(2,1)}), bf16[8,18,16,512]{3,2,1,0:T(8,128)(2,1)S(1)}, u32[]{:S(2)}, u32[]{:S(2)}) %all-to-all-start) | async-done | bytes 2359328 | tf_op jit(solution)/shard_map/all_to_all | solution.py:261
  88.0 0.0 collective-permute-done.2.rest_0_
  88.0 6.0 %own.1 = f32[384,512]{1,0:T(8,128)} custom-call(s32[6,24]{1,0:T(8,128)S(1)} %select_bitcast_fusion.1.slots, bf16[6,128,128]{2,1,0:T(8,128)(2,1)S(1)} %copy-done.2, bf16[144,16,512]{2,1,0:T(8,128)(2,1)S(1)} %bitcast.14, bf16[384,512]{1,0:T(8,128)(2,1)S(1)} %collective-permute-done.2.rest_0_, f32[6,384,512]{2,1,0:T(8,128)} %forward.1.rest_1_, ...), custom_call_target="tpu_custom_call" | custom-call | tf_op jit(solution)/shard_map/own/pallas_call | solution.py:202
  (19 shorter events, 0.1 us)
Async XLA Ops:
  3.2 5.4 %copy-start.7 = (s32[24,6]{0,1:T(8,128)S(1)}, s32[24,6]{0,1:T(8,128)}, u32[]{:S(2)}) copy-start(s32[24,6]{0,1:T(8,128)} %param.7) | copy-start | bytes 1732
  3.3 8.7 %copy-start.6 = (f32[24,16,512]{2,1,0:T(8,128)S(1)}, f32[24,16,512]{2,1,0:T(8,128)}, u32[]{:S(2)}) copy-start(f32[24,16,512]{2,1,0:T(8,128)} %param.5) | copy-start | bytes 2359300
  3.3 8.9 %copy-start.8 = (f32[6,3]{0,1:T(4,128)S(1)}, f32[6,3]{0,1:T(4,128)}, u32[]{:S(2)}) copy-start(f32[6,3]{0,1:T(4,128)} %param.8) | copy-start | bytes 220
  3.3 9.0 %copy-start.9 = (s32[6,3]{0,1:T(4,128)S(1)}, s32[6,3]{0,1:T(4,128)}, u32[]{:S(2)}) copy-start(s32[6,3]{0,1:T(4,128)} %param.9) | copy-start | bytes 220
  3.3 42.5 %all-to-all-start.1 = ((bf16[8,18,16,512]{3,2,1,0:T(8,128)(2,1)}), bf16[8,18,16,512]{3,2,1,0:T(8,128)(2,1)}, u32[]{:S(2)}, u32[]{:S(2)}) async-start(bf16[8,18,16,512]{3,2,1,0:T(8,128)(2,1)} %dynamic-slice_bitcast_fusion), calls=%async_computation.1 | async-start | bytes 4718592 | tf_op jit(solution)/shard_map/all_to_all | solution.py:261
  8.7 26.7 %collective-permute-start.1 = (s32[24,6]{0,1:T(8,128)S(1)}, s32[24,6]{0,1:T(8,128)S(1)}, u32[]{:S(2)}, u32[]{:S(2)}) collective-permute-start(s32[24,6]{0,1:T(8,128)S(1)} %copy-done.7), channel_id=1, source_target_pairs={{0,8},{1,9},{2,10},{3,11},{4,12},{5,13},{6,14},{7,15},{8,0},{9,1},... | collective-permute-start | bytes 1736 | tf_op jit(solution)/shard_map/ppermute | solution.py:267
  11.9 31.7 %collective-permute-start = (bf16[384,512]{1,0:T(8,128)(2,1)S(1)}, bf16[384,512]{1,0:T(8,128)(2,1)}, u32[]{:S(2)}, u32[]{:S(2)}) collective-permute-start(bf16[384,512]{1,0:T(8,128)(2,1)S(1)} %bitcast_convert_fusion.est), channel_id=1, source_target_pairs={{0,8},{1,9},{2,10},{3,11},{4,12},{5,13},{6,14},{7,15},{8,0},{9,1},... | collective-permute-start | bytes 1179656 | tf_op jit(solution)/shard_map/ppermute | solution.py:266
  22.7 0.7 copy-start.1
  23.3 0.7 copy-start.3
  24.0 3.5 %copy-start = (bf16[6,512,512]{2,1,0:T(8,128)(2,1)S(1)}, bf16[6,512,512]{2,1,0:T(8,128)(2,1)}, u32[]{:S(2)}) copy-start(bf16[6,512,512]{2,1,0:T(8,128)(2,1)} %get-tuple-element.17.wf.rest_0_) | copy-start | bytes 9437188
  24.0 3.5 %copy-start.4 = (bf16[6,128,128]{2,1,0:T(8,128)(2,1)S(1)}, bf16[6,128,128]{2,1,0:T(8,128)(2,1)}, u32[]{:S(2)}) copy-start(bf16[6,128,128]{2,1,0:T(8,128)(2,1)} %copy-done.3) | copy-start | bytes 589828
  32.4 18.7 %copy-start.2 = (bf16[6,128,128]{2,1,0:T(8,128)(2,1)S(1)}, bf16[6,128,128]{2,1,0:T(8,128)(2,1)}, u32[]{:S(2)}) copy-start(bf16[6,128,128]{2,1,0:T(8,128)(2,1)} %copy-done.1) | copy-start | bytes 589828
  32.4 18.7 %copy-start.5 = (bf16[6,128,128]{2,1,0:T(8,128)(2,1)S(1)}, bf16[6,128,128]{2,1,0:T(8,128)(2,1)}, u32[]{:S(2)}) copy-start(bf16[6,128,128]{2,1,0:T(8,128)(2,1)} %copy-done.3) | copy-start | bytes 589828
  45.8 42.2 %all-to-all-start = ((bf16[8,18,16,512]{3,2,1,0:T(8,128)(2,1)}), bf16[8,18,16,512]{3,2,1,0:T(8,128)(2,1)S(1)}, u32[]{:S(2)}, u32[]{:S(2)}) async-start(bf16[8,18,16,512]{3,2,1,0:T(8,128)(2,1)} %dynamic-slice_bitcast_fusion.1), calls=%async_computation | async-start | bytes 4718592 | tf_op jit(solution)/shard_map/all_to_all | solution.py:261
  59.0 29.0 %collective-permute-start.2 = (bf16[384,512]{1,0:T(8,128)(2,1)}, bf16[384,512]{1,0:T(8,128)(2,1)S(1)}, u32[]{:S(2)}, u32[]{:S(2)}) collective-permute-start(bf16[384,512]{1,0:T(8,128)(2,1)} %other.1), channel_id=1, source_target_pairs={{0,8},{1,9},{2,10},{3,11},{4,12},{5,13},{6,14},{7,15},{8,0},{9,1},... | collective-permute-start | bytes 1179656 | tf_op jit(solution)/shard_map/ppermute | solution.py:279

commit v3 on v2

--- a/solution.py
+++ b/solution.py
@@ -80,7 +80,7 @@
     p2 = jnp.dot(est[...], wf[0], preferred_element_type=jnp.float32).astype(jnp.bfloat16)
     for g in range(est.shape[0] // size):
         rows = slice(g * size, (g + 1) * size)
-        rb[0, rows] = 1.0 / jnp.dot(zf[0], p2[rows], preferred_element_type=jnp.float32)
+        rb[0, rows] = (1.0 / jnp.dot(zf[0], p2[rows], preferred_element_type=jnp.float32)).astype(rb.dtype)
 
 
 def _forward(est, wf, zf):
@@ -95,7 +95,7 @@
             pl.BlockSpec((1, size, size), lambda v: (v, 0, 0)),
         ],
         out_specs=pl.BlockSpec((1, rows, plane), lambda v: (v, 0, 0)),
-        out_shape=pltpu.HBM((views, rows, plane), jnp.float32),
+        out_shape=pltpu.HBM((views, rows, plane), jnp.bfloat16),
         compiler_params=pltpu.CompilerParams(vmem_limit_bytes=VMEM_LIMIT),
         name="forward",
     )(est, wf, zf)
@@ -182,12 +182,11 @@
     for v in range(views):
         pairs += [(rb_hbm.at[v], rb.at[v]), (wb_hbm.at[v], wb.at[v])]
     copies = _fetch(pairs + [(est_hbm, est)], sems)
-    acc[...] = jnp.ones_like(acc)
+    acc[...] = prior[0][...].astype(jnp.float32)
 
     def finish():
         copies[-1].wait()
-        for factor in (est, *prior):
-            acc[...] = acc[...] * factor[...].astype(jnp.float32)
+        acc[...] = acc[...] * est[...]
 
     _backward_views(
         slots, obs, rb, wb, zb, q1, acc, lambda v: copies[2 * v].wait(), lambda v: copies[2 * v + 1].wait(), finish
@@ -236,6 +235,36 @@
     return _call(kernel, "own", out, slots, whole, (rb, wb), (), (est,), scratch)
 
 
+def _pick_kernel(owners, held, out, buffer, sems_in, sems_out):
+    me = lax.axis_index("tiles")
+    half = out.shape[0]
+    copies = _fetch([(held.at[owners(me, j)], buffer.at[j]) for j in range(half)], sems_in)
+    back = []
+    for j in range(half):
+        copies[j].wait()
+        back.append(pltpu.make_async_copy(buffer.at[j], out.at[j], sems_out.at[j]))
+        back[j].start()
+    for copy in back:
+        copy.wait()
+
+
+def _pick(held, half, owners, name):
+    hbm = pl.BlockSpec(memory_space=pltpu.HBM)
+    shape = (half, *held.shape[1:])
+    return pl.pallas_call(
+        functools.partial(_pick_kernel, owners),
+        in_specs=[hbm],
+        out_specs=hbm,
+        out_shape=pltpu.HBM(shape, held.dtype),
+        scratch_shapes=[
+            pltpu.VMEM(shape, held.dtype),
+            pltpu.SemaphoreType.DMA((half,)),
+            pltpu.SemaphoreType.DMA((half,)),
+        ],
+        name=name,
+    )(held)
+
+
 def _slots(item_tile, first, count, slot_count):
     blocks, views = item_tile.shape
     flat = item_tile.reshape(-1)
@@ -255,8 +284,6 @@
     groups = [list(range(half)), list(range(half, tiles))]
     swap = [(t, (t + half) % tiles) for t in range(tiles)]
 
-    by_half = observed[0].reshape(2, half, slot_count, depth, plane)
-
     def exchange(sent):
         got = lax.all_to_all(sent, "tiles", 0, 0, axis_index_groups=groups, tiled=True)
         return got.reshape(half * slot_count, depth, plane)
@@ -265,13 +292,15 @@
     est_bf = est.astype(jnp.bfloat16)
     est_other = lax.ppermute(est_bf, "tiles", swap)
     item_tile_other = lax.ppermute(item_tile, "tiles", swap)
-    obs_other = exchange(lax.dynamic_index_in_dim(by_half, 1 - mine, 0, keepdims=False))
+    obs_other = exchange(
+        _pick(observed[0], half, lambda me, j: (1 - me // half) * half + j, "pick_other")
+    )
     matrices = _matrices(psf_sigma, view_offsets, depth, plane)
     rb_own = _forward(est_bf, matrices[0], matrices[2])
     slots_own = _slots(item_tile, mine * half, half, slot_count)
     slots_other = _slots(item_tile_other, mine * half, half, slot_count)
-    by_half_2, _ = lax.optimization_barrier((by_half, matrices[2]))
-    sent = lax.dynamic_index_in_dim(by_half_2, mine, 0, keepdims=False)
+    by_half_2, _ = lax.optimization_barrier((observed[0], matrices[2]))
+    sent = _pick(by_half_2, half, lambda me, j: me // half * half + j, "pick_own")
     sent, rb_own, est_other, slots_own, slots_other = lax.optimization_barrier(
         (sent, rb_own, est_other, slots_own, slots_other)
     )

time: 94.3 us -> 93.3 us (0.989)
  local copies, waits for them, and re-layouts: 8.97 us -> 2.81 us
  Pallas kernels: 28.7 us -> 32.7 us
  waiting for transfers between devices: 41.1 us -> 42.3 us
    squeeze x2 -> x0, local copies, waits for them, and re-layouts: 6.69 us -> none  [the longest x1 3.44 us: per_device(): sent = lax.dynamic_index_in_dim(by_half_2, mine, 0, keepdims=False)]
    pallas_call x0 -> x2, Pallas kernels: none -> 5.1 us  [_pick(): pl.pallas_call(functools.partial(_pick_kernel, owners), in_specs=[hbm], o...]
    unnamed x23 -> x13, local copies, waits for them, and re-layouts: 1.65 us -> 2.18 us
  transfers between devices with their start and end apart: 5 -> 5, of which waited for: 4 -> 4; matrix products, arithmetic and copies ran while one was open for 5% -> 1% of each run, Pallas kernels for 24% -> 26%
where the time goes in v3:
time: 93.3 us; the launch traced here: 93 us
  waiting for transfers between devices  42.3 us (45%)
  Pallas kernels  32.7 us (35%)
  starting transfers between devices  14.6 us (16%)
  local copies, waits for them, and re-layouts  2.81 us (3%)
    all_to_all x2, waiting for transfers between devices, exchange(): lax.all_to_all(sent, 'tiles', 0, 0, axis_index_groups=groups, tiled=True)  30.8 us
    pallas_call x2, Pallas kernels, _call(): pl.pallas_call(kernel, in_specs=[smem] + [vmem] * len(whole) + [hbm] * le...  13.2 us
    all_to_all x2, starting transfers between devices, exchange(): lax.all_to_all(sent, 'tiles', 0, 0, axis_index_groups=groups, tiled=True)  10.6 us
    pallas_call x1, Pallas kernels, _matrices(): pl.pallas_call(_matrices_kernel, grid=(views,), in_specs=[smem, smem], ou...  9.89 us
    ppermute x1, waiting for transfers between devices, per_device(): est_other = lax.ppermute(est_bf, 'tiles', swap)  7.65 us
    pallas_call x2, Pallas kernels, _pick(): pl.pallas_call(functools.partial(_pick_kernel, owners), in_specs=[hbm], o...  5.1 us
    pallas_call x1, Pallas kernels, _forward(): pl.pallas_call(_forward_kernel, grid=(views,), in_specs=[pl.BlockSpec((ro...  4.52 us
    ppermute x1, waiting for transfers between devices, per_device(): item_tile_other = lax.ppermute(item_tile, 'tiles', swap)  3.77 us
  transfers between devices with their start and end apart: 5, of which 4 were waited for; matrix products, arithmetic and copies ran while one was open for 1% of the time, Pallas kernels for 26%

profile of v3, /device:TPU:0, one launch (start us, length us, event | category | flops | bytes accessed | tf_op | source)
XLA Modules:
  0.0 93.0 jit_solution(15229937316229359830)
XLA Ops:
  0.0 2.6 %pick_other.1 = bf16[8,18,16,512]{3,2,1,0:T(8,128)(2,1)} custom-call(bf16[16,18,16,512]{3,2,1,0:T(8,128)(2,1)} %bitcast.11), custom_call_target="tpu_custom_call" | custom-call | tf_op jit(solution)/shard_map/pick_other/pallas_call | solution.py:254
  2.6 0.0 copy-start.2
  2.6 0.0 copy-start.1
  2.6 0.0 copy-start.3
  2.7 0.0 copy-start.4
  2.7 5.4 %all-to-all-start.1 = ((bf16[8,18,16,512]{3,2,1,0:T(8,128)(2,1)}), bf16[8,18,16,512]{3,2,1,0:T(8,128)(2,1)}, u32[]{:S(2)}, u32[]{:S(2)}) async-start(bf16[8,18,16,512]{3,2,1,0:T(8,128)(2,1)} %pick_other.1), calls=%async_computation.1 | async-start | bytes 4718592 | tf_op jit(solution)/shard_map/all_to_all | solution.py:288
  8.1 3.2 %collective-permute-start.1 = (s32[24,6]{0,1:T(8,128)S(1)}, s32[24,6]{0,1:T(8,128)S(1)}, u32[]{:S(2)}, u32[]{:S(2)}) collective-permute-start(s32[24,6]{0,1:T(8,128)S(1)} %copy-done.2), channel_id=1, source_target_pairs={{0,8},{1,9},{2,10},{3,11},{4,12},{5,13},{6,14},{7,15},{8,0},{9,1},... | collective-permute-start | bytes 1736 | tf_op jit(solution)/shard_map/ppermute | solution.py:294
  11.4 0.1 collective-permute-start
  11.5 0.1 copy.16
  11.5 0.1 eq.30
  11.6 0.2 convert_reduce_fusion.1
  11.8 0.1 reduce_sum.23
  11.9 0.1 copy.17
  12.0 0.1 copy.14.sigma
  12.1 0.1 copy.15.offset
  12.2 9.9 %matrices.1 = (bf16[6,512,512]{2,1,0:T(8,128)(2,1)}, bf16[6,512,512]{2,1,0:T(8,128)(2,1)}, bf16[6,128,128]{2,1,0:T(8,128)(2,1)S(1)}, bf16[6,128,128]{2,1,0:T(8,128)(2,1)S(1)}) custom-call(f32[6,3]{1,0:T(8,128)S(1)} %copy.14.sigma, s32[6,3]{1,0:T(8,128)S(1)} %copy.15.offset), custom_call_target="tpu_custom_call" | custom-call | tf_op jit(solution)/shard_map/matrices/pallas_call | solution.py:57
  22.1 1.9 %copy-done = bf16[6,512,512]{2,1,0:T(8,128)(2,1)S(1)} copy-done((bf16[6,512,512]{2,1,0:T(8,128)(2,1)S(1)}, bf16[6,512,512]{2,1,0:T(8,128)(2,1)}, u32[]{:S(2)}) %copy-start) | copy-done | bytes 3145752
  24.0 4.5 %forward.1.rest_1_ = bf16[6,384,512]{2,1,0:T(8,128)(2,1)} custom-call(bf16[384,512]{1,0:T(8,128)(2,1)S(1)} %bitcast_convert_fusion.est, bf16[6,512,512]{2,1,0:T(8,128)(2,1)S(1)} %copy-done, bf16[6,128,128]{2,1,0:T(8,128)(2,1)S(1)} %get-tuple-element.15.zf), custom_call_target="tpu_custom_call" | custom-call | tf_op jit(solution)/shard_map/forward/pallas_call | solution.py:89
  28.5 2.5 %pick_own.1 = bf16[8,18,16,512]{3,2,1,0:T(8,128)(2,1)} custom-call(bf16[16,18,16,512]{3,2,1,0:T(8,128)(2,1)} %bitcast.12), custom_call_target="tpu_custom_call" | custom-call | tf_op jit(solution)/shard_map/pick_own/pallas_call | solution.py:254
  31.0 3.8 %collective-permute-done.1 = s32[24,6]{0,1:T(8,128)S(1)} collective-permute-done((s32[24,6]{0,1:T(8,128)S(1)}, s32[24,6]{0,1:T(8,128)S(1)}, u32[]{:S(2)}, u32[]{:S(2)}) %collective-permute-start.1) | collective-permute-done | bytes 608 | tf_op jit(solution)/shard_map/ppermute | solution.py:294
  34.8 0.1 copy.18
  34.9 0.1 eq.34
  35.0 0.2 convert_reduce_fusion
  35.2 0.1 reduce_sum.25
  35.3 0.1 copy.19
  35.4 7.7 %collective-permute-done.est = bf16[384,512]{1,0:T(8,128)(2,1)S(1)} collective-permute-done((bf16[384,512]{1,0:T(8,128)(2,1)S(1)}, bf16[384,512]{1,0:T(8,128)(2,1)S(1)}, u32[]{:S(2)}, u32[]{:S(2)}) %collective-permute-start) | collective-permute-done | bytes 393248 | tf_op jit(solution)/shard_map/ppermute | solution.py:293
  43.0 2.2 %all-to-all-done.1 = bf16[8,18,16,512]{3,2,1,0:T(8,128)(2,1)} async-done(((bf16[8,18,16,512]{3,2,1,0:T(8,128)(2,1)}), bf16[8,18,16,512]{3,2,1,0:T(8,128)(2,1)}, u32[]{:S(2)}, u32[]{:S(2)}) %all-to-all-start.1) | async-done | bytes 2359328 | tf_op jit(solution)/shard_map/all_to_all | solution.py:288
  45.2 5.2 %all-to-all-start = ((bf16[8,18,16,512]{3,2,1,0:T(8,128)(2,1)}), bf16[8,18,16,512]{3,2,1,0:T(8,128)(2,1)S(1)}, u32[]{:S(2)}, u32[]{:S(2)}) async-start(bf16[8,18,16,512]{3,2,1,0:T(8,128)(2,1)} %pick_own.1), calls=%async_computation | async-start | bytes 4718592 | tf_op jit(solution)/shard_map/all_to_all | solution.py:288
  50.4 7.5 %other.1 = bf16[384,512]{1,0:T(8,128)(2,1)} custom-call(s32[6,24]{1,0:T(8,128)S(1)} %select_bitcast_fusion.slots, bf16[384,512]{1,0:T(8,128)(2,1)S(1)} %collective-permute-done.est, bf16[6,128,128]{2,1,0:T(8,128)(2,1)S(1)} %get-tuple-element.15.zf, bf16[6,128,128]{2,1,0:T(8,128)(2,1)S(1)} %get-tuple-element.19.zb, ...), custom_call_target="tpu_custom_call" | custom-call | tf_op jit(solution)/shard_map/other/pallas_call | solution.py:201
  57.9 0.8 collective-permute-start.2
  58.6 28.7 %all-to-all-done = bf16[8,18,16,512]{3,2,1,0:T(8,128)(2,1)S(1)} async-done(((bf16[8,18,16,512]{3,2,1,0:T(8,128)(2,1)}), bf16[8,18,16,512]{3,2,1,0:T(8,128)(2,1)S(1)}, u32[]{:S(2)}, u32[]{:S(2)}) %all-to-all-start) | async-done | bytes 2359328 | tf_op jit(solution)/shard_map/all_to_all | solution.py:288
  87.3 5.7 %own.1 = f32[384,512]{1,0:T(8,128)} custom-call(s32[6,24]{1,0:T(8,128)S(1)} %select_bitcast_fusion.1.slots, bf16[6,128,128]{2,1,0:T(8,128)(2,1)S(1)} %get-tuple-element.19.zb, bf16[144,16,512]{2,1,0:T(8,128)(2,1)S(1)} %bitcast.10, bf16[384,512]{1,0:T(8,128)(2,1)S(1)} %collective-permute-done.2.rest_0_, bf16[6,384,512]{2,1,0:T(8,128)(2,1)} %forward.1.rest_1_, ...), custom_call_target="tpu_custom_call" | custom-call | tf_op jit(solution)/shard_map/own/pallas_call | solution.py:201
  (9 shorter events, 0.1 us)
Async XLA Ops:
  2.6 5.5 %copy-start.2 = (s32[24,6]{0,1:T(8,128)S(1)}, s32[24,6]{0,1:T(8,128)}, u32[]{:S(2)}) copy-start(s32[24,6]{0,1:T(8,128)} %param.7) | copy-start | bytes 1732
  2.6 8.7 %copy-start.1 = (f32[24,16,512]{2,1,0:T(8,128)S(1)}, f32[24,16,512]{2,1,0:T(8,128)}, u32[]{:S(2)}) copy-start(f32[24,16,512]{2,1,0:T(8,128)} %param.5) | copy-start | bytes 2359300
  2.6 9.4 %copy-start.3 = (f32[6,3]{0,1:T(4,128)S(1)}, f32[6,3]{0,1:T(4,128)}, u32[]{:S(2)}) copy-start(f32[6,3]{0,1:T(4,128)} %param.8) | copy-start | bytes 220
  2.7 9.5 %copy-start.4 = (s32[6,3]{0,1:T(4,128)S(1)}, s32[6,3]{0,1:T(4,128)}, u32[]{:S(2)}) copy-start(s32[6,3]{0,1:T(4,128)} %param.9) | copy-start | bytes 220
  2.7 42.5 %all-to-all-start.1 = ((bf16[8,18,16,512]{3,2,1,0:T(8,128)(2,1)}), bf16[8,18,16,512]{3,2,1,0:T(8,128)(2,1)}, u32[]{:S(2)}, u32[]{:S(2)}) async-start(bf16[8,18,16,512]{3,2,1,0:T(8,128)(2,1)} %pick_other.1), calls=%async_computation.1 | async-start | bytes 4718592 | tf_op jit(solution)/shard_map/all_to_all | solution.py:288
  8.1 26.7 %collective-permute-start.1 = (s32[24,6]{0,1:T(8,128)S(1)}, s32[24,6]{0,1:T(8,128)S(1)}, u32[]{:S(2)}, u32[]{:S(2)}) collective-permute-start(s32[24,6]{0,1:T(8,128)S(1)} %copy-done.2), channel_id=1, source_target_pairs={{0,8},{1,9},{2,10},{3,11},{4,12},{5,13},{6,14},{7,15},{8,0},{9,1},... | collective-permute-start | bytes 1736 | tf_op jit(solution)/shard_map/ppermute | solution.py:294
  11.4 31.6 %collective-permute-start = (bf16[384,512]{1,0:T(8,128)(2,1)S(1)}, bf16[384,512]{1,0:T(8,128)(2,1)S(1)}, u32[]{:S(2)}, u32[]{:S(2)}) collective-permute-start(bf16[384,512]{1,0:T(8,128)(2,1)S(1)} %bitcast_convert_fusion.est), channel_id=1, source_target_pairs={{0,8},{1,9},{2,10},{3,11},{4,12},{5,13},{6,14},{7,15},{8,0},{9,1},... | collective-permute-start | bytes 1179656 | tf_op jit(solution)/shard_map/ppermute | solution.py:293
  22.1 1.9 %copy-start = (bf16[6,512,512]{2,1,0:T(8,128)(2,1)S(1)}, bf16[6,512,512]{2,1,0:T(8,128)(2,1)}, u32[]{:S(2)}) copy-start(bf16[6,512,512]{2,1,0:T(8,128)(2,1)} %get-tuple-element.17.wf.rest_0_) | copy-start | bytes 9437188
  45.2 42.1 %all-to-all-start = ((bf16[8,18,16,512]{3,2,1,0:T(8,128)(2,1)}), bf16[8,18,16,512]{3,2,1,0:T(8,128)(2,1)S(1)}, u32[]{:S(2)}, u32[]{:S(2)}) async-start(bf16[8,18,16,512]{3,2,1,0:T(8,128)(2,1)} %pick_own.1), calls=%async_computation | async-start | bytes 4718592 | tf_op jit(solution)/shard_map/all_to_all | solution.py:288
  57.9 29.4 %collective-permute-start.2 = (bf16[384,512]{1,0:T(8,128)(2,1)}, bf16[384,512]{1,0:T(8,128)(2,1)S(1)}, u32[]{:S(2)}, u32[]{:S(2)}) collective-permute-start(bf16[384,512]{1,0:T(8,128)(2,1)} %other.1), channel_id=1, source_target_pairs={{0,8},{1,9},{2,10},{3,11},{4,12},{5,13},{6,14},{7,15},{8,0},{9,1},... | collective-permute-start | bytes 1179656 | tf_op jit(solution)/shard_map/ppermute | solution.py:308

commit v4 on v3

--- a/solution.py
+++ b/solution.py
@@ -12,6 +12,7 @@
 TAP_REACH = 15
 GROUP = 8
 VMEM_LIMIT = 28 << 20
+OTHER_COST = pl.CostEstimate(flops=30 * 10**9, transcendentals=0, bytes_accessed=100 << 20)
 
 
 def _table(sigma, offset, n, transposed):
@@ -163,7 +164,7 @@
     for v in range(views + 1):
         if v < views:
             copies[v].wait()
-            p2[v] = jnp.dot(est[...], wf[v], preferred_element_type=jnp.float32).astype(jnp.bfloat16)
+            p2[v] = jnp.dot(est[: rb.shape[1]], wf[v], preferred_element_type=jnp.float32).astype(jnp.bfloat16)
         if v > 0:
             for span in _spans(rb.shape[1], size):
                 rb[v - 1, span] = 1.0 / jnp.dot(zf[v - 1], p2[v - 1, span], preferred_element_type=jnp.float32)
@@ -193,7 +194,7 @@
     )
 
 
-def _call(kernel, name, out_shape, slots, whole, far, obs, near, scratch):
+def _call(kernel, name, out_shape, slots, whole, far, obs, near, scratch, cost=None):
     count = sum(o.shape[0] for o in obs)
     smem, vmem, hbm = (pl.BlockSpec(memory_space=m) for m in (pltpu.SMEM, pltpu.VMEM, pltpu.HBM))
     fetched = (*far, *obs, *near)
@@ -209,13 +210,14 @@
         + scratch
         + [pltpu.SemaphoreType.DMA((n_copies,))],
         compiler_params=pltpu.CompilerParams(vmem_limit_bytes=VMEM_LIMIT),
+        cost_estimate=cost,
         name=name,
     )(slots, *whole, *(pltpu.with_memory_space_constraint(x, pltpu.HBM) for x in fetched))
 
 
 def _other(slots, est, obs, matrices, prior=()):
     wf, wb, zf, zb = matrices
-    rows, plane = est.shape
+    rows, plane = slots.shape[1] * obs[0].shape[1], est.shape[1]
     scratch = [
         pltpu.VMEM((wf.shape[0], rows, plane), jnp.bfloat16),
         pltpu.VMEM((wf.shape[0], rows, plane), jnp.float32),
@@ -223,7 +225,7 @@
     ]
     kernel = functools.partial(_other_kernel, len(obs), len(prior))
     out = pltpu.HBM((rows, plane), jnp.bfloat16)
-    return _call(kernel, "other", out, slots, (est, zf, zb, *prior), (wf, wb), obs, (), scratch)
+    return _call(kernel, "other", out, slots, (est, zf, zb, *prior), (wf, wb), obs, (), scratch, OTHER_COST)
 
 
 def _own(slots, est, obs, rb, matrices, prior):
@@ -235,29 +237,30 @@
     return _call(kernel, "own", out, slots, whole, (rb, wb), (), (est,), scratch)
 
 
-def _pick_kernel(owners, held, out, buffer, sems_in, sems_out):
+def _pick_kernel(owners, held, *rest):
+    *outs, buffer, sems_in, sems_out = rest
     me = lax.axis_index("tiles")
-    half = out.shape[0]
+    half = buffer.shape[0]
     copies = _fetch([(held.at[owners(me, j)], buffer.at[j]) for j in range(half)], sems_in)
-    back = []
+    back, places = [], [out.at[n] for out in outs for n in range(out.shape[0])]
     for j in range(half):
         copies[j].wait()
-        back.append(pltpu.make_async_copy(buffer.at[j], out.at[j], sems_out.at[j]))
+        back.append(pltpu.make_async_copy(buffer.at[j], places[j], sems_out.at[j]))
         back[j].start()
     for copy in back:
         copy.wait()
 
 
-def _pick(held, half, owners, name):
+def _pick(held, counts, owners, name):
     hbm = pl.BlockSpec(memory_space=pltpu.HBM)
-    shape = (half, *held.shape[1:])
+    half = sum(counts)
     return pl.pallas_call(
         functools.partial(_pick_kernel, owners),
         in_specs=[hbm],
-        out_specs=hbm,
-        out_shape=pltpu.HBM(shape, held.dtype),
+        out_specs=[hbm] * len(counts),
+        out_shape=[pltpu.HBM((count, *held.shape[1:]), held.dtype) for count in counts],
         scratch_shapes=[
-            pltpu.VMEM(shape, held.dtype),
+            pltpu.VMEM((half, *held.shape[1:]), held.dtype),
             pltpu.SemaphoreType.DMA((half,)),
             pltpu.SemaphoreType.DMA((half,)),
         ],
@@ -265,47 +268,63 @@
     )(held)
 
 
-def _slots(item_tile, first, count, slot_count):
+def _slots(item_tile, first, count, slot_count, place=lambda tile: tile):
     blocks, views = item_tile.shape
     flat = item_tile.reshape(-1)
     order = jnp.arange(blocks * views, dtype=jnp.int32)
     before = (flat[:, None] == flat[None, :]) & (order[None, :] < order[:, None])
     rank = jnp.sum(before.astype(jnp.int32), axis=1)
     tile = flat - first
-    slot = jnp.where((tile >= 0) & (tile < count), tile * slot_count + rank, -1)
+    slot = jnp.where((tile >= 0) & (tile < count), place(tile) * slot_count + rank, -1)
     return slot.reshape(blocks, views).T
 
 
 def per_device(estimate, observed, item_tile, psf_sigma, view_offsets):
     blocks, depth, plane = estimate.shape
     tiles, slot_count = observed.shape[1:3]
-    half = tiles // 2
-    mine = lax.axis_index("tiles") // half
-    groups = [list(range(half)), list(range(half, tiles))]
+    views = item_tile.shape[1]
+    half, quarter = tiles // 2, tiles // 4
+    me = lax.axis_index("tiles")
+    mine, side, turn = me // half, me // quarter % 2, me % quarter
+    halves = [list(range(first, first + half)) for first in range(0, tiles, half)]
+    quarters = [list(range(first, first + quarter)) for first in range(0, tiles, quarter)]
     swap = [(t, (t + half) % tiles) for t in range(tiles)]
 
-    def exchange(sent):
+    def exchange(sent, groups):
         got = lax.all_to_all(sent, "tiles", 0, 0, axis_index_groups=groups, tiled=True)
-        return got.reshape(half * slot_count, depth, plane)
+        return got.reshape(-1, depth, plane)
+
+    def owner(me, j):
+        near = me // quarter % 2 * quarter + j
+        across = (1 - me // quarter % 2) * quarter + (me + j) % quarter
+        return (1 - me // half) * half + (near if j < quarter else across)
+
+    def place(tile):
+        return jnp.where(tile // quarter == side, tile % quarter, quarter + (turn - tile % quarter + quarter) % quarter)
 
     est = estimate.reshape(blocks * depth, plane)
     est_bf = est.astype(jnp.bfloat16)
-    est_other = lax.ppermute(est_bf, "tiles", swap)
-    item_tile_other = lax.ppermute(item_tile, "tiles", swap)
-    obs_other = exchange(
-        _pick(observed[0], half, lambda me, j: (1 - me // half) * half + j, "pick_other")
-    )
+    names = item_tile.reshape(-1).astype(jnp.bfloat16)
+    names = jnp.pad(names, (0, depth * plane - names.shape[0])).reshape(depth, plane)
+    est_other = lax.ppermute(jnp.concatenate([est_bf, names], axis=0), "tiles", swap)
+    near, *across = _pick(observed[0], [quarter] + [1] * quarter, owner, "pick_other")
+    obs_near = exchange(near, quarters)
+    obs_across = []
+    for d, sent in enumerate(across):
+        ring = [(t, (t // quarter ^ 1) * quarter + (t + d) % quarter) for t in range(tiles)]
+        obs_across.append(lax.ppermute(sent, "tiles", ring).reshape(slot_count, depth, plane))
+
     matrices = _matrices(psf_sigma, view_offsets, depth, plane)
     rb_own = _forward(est_bf, matrices[0], matrices[2])
     slots_own = _slots(item_tile, mine * half, half, slot_count)
-    slots_other = _slots(item_tile_other, mine * half, half, slot_count)
-    by_half_2, _ = lax.optimization_barrier((observed[0], matrices[2]))
-    sent = _pick(by_half_2, half, lambda me, j: me // half * half + j, "pick_own")
-    sent, rb_own, est_other, slots_own, slots_other = lax.optimization_barrier(
-        (sent, rb_own, est_other, slots_own, slots_other)
-    )
-    obs_own = exchange(sent)
-    product = lax.ppermute(_other(slots_other, est_other, [obs_other], matrices), "tiles", swap)
+    held, _ = lax.optimization_barrier((observed[0], matrices[2]))
+    (own,) = _pick(held, [half], lambda me, j: me // half * half + j, "pick_own")
+    own, rb_own, slots_own, obs_near = lax.optimization_barrier((own, rb_own, slots_own, obs_near))
+    obs_own = exchange(own, halves)
+    item_tile_other = est_other[blocks * depth :].reshape(-1)[: blocks * views].astype(jnp.int32).reshape(blocks, views)
+    slots_other = _slots(item_tile_other, mine * half, half, slot_count, place)
+    sent_back = _other(slots_other, est_other, [obs_near, *obs_across], matrices)
+    product = lax.ppermute(sent_back, "tiles", swap)
     updated = _own(slots_own, est, obs_own, rb_own, matrices, [product])
     return updated.reshape(blocks, depth, plane)
 

time: 93.3 us -> 87.1 us (0.934)
  waiting for transfers between devices: 42.3 us -> 29.5 us
  starting transfers between devices: 14.6 us -> 19.1 us
  local copies, waits for them, and re-layouts: 2.81 us -> 3.84 us
    all_to_all x2, waiting for transfers between devices: 30.8 us -> 0.89 us  [exchange(): lax.all_to_all(sent, 'tiles', 0, 0, axis_index_groups=groups, tiled=True)]
    ppermute x3 -> x6, waiting for transfers between devices: 11.4 us -> 28.6 us  [the longest x1 23.8 us: per_device(): product = lax.ppermute(sent_back, 'tiles', swap)]
    ppermute x3 -> x6, starting transfers between devices: 4.08 us -> 11.1 us  [the longest x4 5.81 us: per_device(): lax.ppermute(sent, 'tiles', ring).reshape(slot_count, depth, plane)]
    all_to_all x2, starting transfers between devices: 10.6 us -> 7.99 us  [exchange(): lax.all_to_all(sent, 'tiles', 0, 0, axis_index_groups=groups, tiled=True)]
    unnamed x13 -> x17, local copies, waits for them, and re-layouts: 2.18 us -> 3.18 us
  transfers between devices with their start and end apart: 5 -> 8, of which waited for: 4 -> 4; matrix products, arithmetic and copies ran while one was open for 1% -> 3% of each run, Pallas kernels for 26% -> 28%
where the time goes in v4:
time: 87.1 us; the launch traced here: 86.8 us
  Pallas kernels  32.8 us (38%)
  waiting for transfers between devices  29.5 us (34%)
  starting transfers between devices  19.1 us (22%)
  local copies, waits for them, and re-layouts  3.84 us (4%)
  other arithmetic  1.26 us (1%)
    ppermute x1, waiting for transfers between devices, per_device(): product = lax.ppermute(sent_back, 'tiles', swap)  23.8 us
    pallas_call x2, Pallas kernels, _call(): pl.pallas_call(kernel, in_specs=[smem] + [vmem] * len(whole) + [hbm] * le...  13.2 us
    pallas_call x1, Pallas kernels, _matrices(): pl.pallas_call(_matrices_kernel, grid=(views,), in_specs=[smem, smem], ou...  9.89 us
    all_to_all x2, starting transfers between devices, exchange(): lax.all_to_all(sent, 'tiles', 0, 0, axis_index_groups=groups, tiled=True)  7.99 us
    ppermute x4, starting transfers between devices, per_device(): lax.ppermute(sent, 'tiles', ring).reshape(slot_count, depth, plane)  5.81 us
    pallas_call x2, Pallas kernels, _pick(): pl.pallas_call(functools.partial(_pick_kernel, owners), in_specs=[hbm], o...  5.19 us
    ppermute x4, waiting for transfers between devices, per_device(): lax.ppermute(sent, 'tiles', ring).reshape(slot_count, depth, plane)  4.76 us
    pallas_call x1, Pallas kernels, _forward(): pl.pallas_call(_forward_kernel, grid=(views,), in_specs=[pl.BlockSpec((ro...  4.57 us
  transfers between devices with their start and end apart: 8, of which 4 were waited for; matrix products, arithmetic and copies ran while one was open for 3% of the time, Pallas kernels for 28%

profile of v4, /device:TPU:0, one launch (start us, length us, event | category | flops | bytes accessed | tf_op | source)
XLA Modules:
  0.0 86.8 jit_solution(13072072182586723536)
XLA Ops:
  0.0 2.6 %pick_other.1 = (bf16[4,18,16,512]{3,2,1,0:T(8,128)(2,1)}, bf16[1,18,16,512]{3,2,1,0:T(8,128)(2,1)}, bf16[1,18,16,512]{3,2,1,0:T(8,128)(2,1)}, bf16[1,18,16,512]{3,2,1,0:T(8,128)(2,1)}, bf16[1,18,16,512]{3,2,1,0:T(8,128)(2,1)}) custom-call(bf16[16,18,16,512]{3,2,1,0:T(8,128)(2,1)} %bitcast.18), custom_call_target="tpu_custom_call" | custom-call | tf_op jit(solution)/shard_map/pick_other/pallas_call | solution.py:257
  2.7 4.4 %all-to-all-start = ((bf16[4,18,16,512]{3,2,1,0:T(8,128)(2,1)}), bf16[4,18,16,512]{3,2,1,0:T(8,128)(2,1)S(1)}, u32[]{:S(2)}, u32[]{:S(2)}) async-start(bf16[4,18,16,512]{3,2,1,0:T(8,128)(2,1)} %get-tuple-element.22), calls=%async_computation | async-start | bytes 2359296 | tf_op jit(solution)/shard_map/all_to_all | solution.py:294
  7.0 0.1 copy.21
  7.1 0.1 eq.42
  7.3 0.8 pad_maximum_fusion
  8.1 3.3 %collective-permute-start = (bf16[400,512]{1,0:T(8,128)(2,1)}, bf16[400,512]{1,0:T(8,128)(2,1)S(1)}, u32[]{:S(2)}, u32[]{:S(2)}) collective-permute-start(bf16[400,512]{1,0:T(8,128)(2,1)} %pad_maximum_fusion), channel_id=1, source_target_pairs={{0,8},{1,9},{2,10},{3,11},{4,12},{5,13},{6,14},{7,15},{8,0},{9,1},... | collective-permute-start | bytes 1228808 | tf_op jit(solution)/shard_map/ppermute | solution.py:309
  11.5 1.6 %collective-permute-start.1 = (bf16[1,18,16,512]{3,2,1,0:T(8,128)(2,1)}, bf16[1,18,16,512]{3,2,1,0:T(8,128)(2,1)}, u32[]{:S(2)}, u32[]{:S(2)}) collective-permute-start(bf16[1,18,16,512]{3,2,1,0:T(8,128)(2,1)} %get-tuple-element.28), channel_id=1, source_target_pairs={{0,4},{1,5},{2,6},{3,7},{4,0},{5,1},{6,2},{7,3},{8,12},{9,13},{10,... | collective-permute-start | bytes 884744 | tf_op jit(solution)/shard_map/ppermute | solution.py:315
  13.0 2.6 %collective-permute-start.3 = (bf16[1,18,16,512]{3,2,1,0:T(8,128)(2,1)}, bf16[1,18,16,512]{3,2,1,0:T(8,128)(2,1)}, u32[]{:S(2)}, u32[]{:S(2)}) collective-permute-start(bf16[1,18,16,512]{3,2,1,0:T(8,128)(2,1)} %get-tuple-element.30), channel_id=1, source_target_pairs={{0,6},{1,7},{2,4},{3,5},{4,2},{5,3},{6,0},{7,1},{8,14},{9,15},{10,... | collective-permute-start | bytes 884744 | tf_op jit(solution)/shard_map/ppermute | solution.py:315
  15.7 1.6 %collective-permute-start.4 = (bf16[1,18,16,512]{3,2,1,0:T(8,128)(2,1)}, bf16[1,18,16,512]{3,2,1,0:T(8,128)(2,1)}, u32[]{:S(2)}, u32[]{:S(2)}) collective-permute-start(bf16[1,18,16,512]{3,2,1,0:T(8,128)(2,1)} %get-tuple-element.31), channel_id=1, source_target_pairs={{0,7},{1,4},{2,5},{3,6},{4,3},{5,0},{6,1},{7,2},{8,15},{9,12},{10,... | collective-permute-start | bytes 884744 | tf_op jit(solution)/shard_map/ppermute | solution.py:315
  17.3 0.1 copy.19.sigma
  17.4 0.1 copy.20.offset
  17.5 0.2 convert_reduce_fusion.1
  17.7 0.1 reduce_sum.23
  17.8 0.1 copy.22
  17.8 9.9 %matrices.1 = (bf16[6,512,512]{2,1,0:T(8,128)(2,1)}, bf16[6,512,512]{2,1,0:T(8,128)(2,1)}, bf16[6,128,128]{2,1,0:T(8,128)(2,1)S(1)}, bf16[6,128,128]{2,1,0:T(8,128)(2,1)S(1)}) custom-call(f32[6,3]{1,0:T(8,128)S(1)} %copy.19.sigma, s32[6,3]{1,0:T(8,128)S(1)} %copy.20.offset), custom_call_target="tpu_custom_call" | custom-call | tf_op jit(solution)/shard_map/matrices/pallas_call | solution.py:58
  27.7 1.9 %copy-done = bf16[6,512,512]{2,1,0:T(8,128)(2,1)S(1)} copy-done((bf16[6,512,512]{2,1,0:T(8,128)(2,1)S(1)}, bf16[6,512,512]{2,1,0:T(8,128)(2,1)}, u32[]{:S(2)}) %copy-start) | copy-done | bytes 3145752
  29.6 4.6 %forward.1.rest_1_ = bf16[6,384,512]{2,1,0:T(8,128)(2,1)} custom-call(bf16[384,512]{1,0:T(8,128)(2,1)S(1)} %bitcast_convert_fusion.est, bf16[6,512,512]{2,1,0:T(8,128)(2,1)S(1)} %copy-done, bf16[6,128,128]{2,1,0:T(8,128)(2,1)S(1)} %get-tuple-element.19.zf), custom_call_target="tpu_custom_call" | custom-call | tf_op jit(solution)/shard_map/forward/pallas_call | solution.py:90
  34.2 2.6 %pick_own.1 = bf16[8,18,16,512]{3,2,1,0:T(8,128)(2,1)} custom-call(bf16[16,18,16,512]{3,2,1,0:T(8,128)(2,1)} %bitcast.19), custom_call_target="tpu_custom_call" | custom-call | tf_op jit(solution)/shard_map/pick_own/pallas_call | solution.py:257
  36.8 1.0 %copy-done.2 = bf16[4,18,16,512]{3,2,1,0:T(8,128)(2,1)} copy-done((bf16[4,18,16,512]{3,2,1,0:T(8,128)(2,1)}, bf16[4,18,16,512]{3,2,1,0:T(8,128)(2,1)S(1)}, u32[]{:S(2)}) %copy-start.2) | copy-done | bytes 1179672
  37.8 3.6 %all-to-all-start.1 = ((bf16[8,18,16,512]{3,2,1,0:T(8,128)(2,1)}), bf16[8,18,16,512]{3,2,1,0:T(8,128)(2,1)S(1)}, u32[]{:S(2)}, u32[]{:S(2)}) async-start(bf16[8,18,16,512]{3,2,1,0:T(8,128)(2,1)} %pick_own.1), calls=%async_computation.1 | async-start | bytes 4718592 | tf_op jit(solution)/shard_map/all_to_all | solution.py:294
  41.5 0.2 convert_reduce_fusion
  41.7 0.1 reduce_sum.25
  41.8 0.1 copy.29
  41.9 0.1 sub.42
  42.0 0.1 copy.23
  42.1 1.2 %collective-permute-done.3 = bf16[1,18,16,512]{3,2,1,0:T(8,128)(2,1)} collective-permute-done((bf16[1,18,16,512]{3,2,1,0:T(8,128)(2,1)}, bf16[1,18,16,512]{3,2,1,0:T(8,128)(2,1)}, u32[]{:S(2)}, u32[]{:S(2)}) %collective-permute-start.3) | collective-permute-done | bytes 294944 | tf_op jit(solution)/shard_map/ppermute | solution.py:315
  43.3 3.6 %collective-permute-done.4 = bf16[1,18,16,512]{3,2,1,0:T(8,128)(2,1)} collective-permute-done((bf16[1,18,16,512]{3,2,1,0:T(8,128)(2,1)}, bf16[1,18,16,512]{3,2,1,0:T(8,128)(2,1)}, u32[]{:S(2)}, u32[]{:S(2)}) %collective-permute-start.4) | collective-permute-done | bytes 294944 | tf_op jit(solution)/shard_map/ppermute | solution.py:315
  46.9 7.5 %other.1 = bf16[384,512]{1,0:T(8,128)(2,1)} custom-call(s32[6,24]{1,0:T(8,128)S(1)} %fusion.9.slots, bf16[400,512]{1,0:T(8,128)(2,1)S(1)} %collective-permute-done.est, bf16[6,128,128]{2,1,0:T(8,128)(2,1)S(1)} %get-tuple-element.19.zf, bf16[6,128,128]{2,1,0:T(8,128)(2,1)S(1)} %get-tuple-element.24.zb, bf16[6,512,512]{2,1,0:T(8,128)(2,1)} %get-tuple-element.21.wf.rest_0_, ...), custom_call_target="tpu_custom_call" | custom-call | flops 30000001024 | bytes 104857600 | tf_op jit(solution)/shard_map/other/pallas_call | solution.py:202
  54.4 2.0 %collective-permute-start.5 = (bf16[384,512]{1,0:T(8,128)(2,1)}, bf16[384,512]{1,0:T(8,128)(2,1)S(1)}, u32[]{:S(2)}, u32[]{:S(2)}) collective-permute-start(bf16[384,512]{1,0:T(8,128)(2,1)} %other.1), channel_id=1, source_target_pairs={{0,8},{1,9},{2,10},{3,11},{4,12},{5,13},{6,14},{7,15},{8,0},{9,1},... | collective-permute-start | bytes 1179656 | tf_op jit(solution)/shard_map/ppermute | solution.py:327
  56.4 23.8 %collective-permute-done.5.rest_0_ = bf16[384,512]{1,0:T(8,128)(2,1)S(1)} collective-permute-done((bf16[384,512]{1,0:T(8,128)(2,1)}, bf16[384,512]{1,0:T(8,128)(2,1)S(1)}, u32[]{:S(2)}, u32[]{:S(2)}) %collective-permute-start.5) | collective-permute-done | bytes 393248 | tf_op jit(solution)/shard_map/ppermute | solution.py:327
  80.2 0.9 %all-to-all-done.1 = bf16[8,18,16,512]{3,2,1,0:T(8,128)(2,1)S(1)} async-done(((bf16[8,18,16,512]{3,2,1,0:T(8,128)(2,1)}), bf16[8,18,16,512]{3,2,1,0:T(8,128)(2,1)S(1)}, u32[]{:S(2)}, u32[]{:S(2)}) %all-to-all-start.1) | async-done | bytes 2359328 | tf_op jit(solution)/shard_map/all_to_all | solution.py:294
  81.1 5.7 %own.1 = f32[384,512]{1,0:T(8,128)} custom-call(s32[6,24]{1,0:T(8,128)S(1)} %select_bitcast_fusion.slots, bf16[6,128,128]{2,1,0:T(8,128)(2,1)S(1)} %get-tuple-element.24.zb, bf16[144,16,512]{2,1,0:T(8,128)(2,1)S(1)} %bitcast.17, bf16[384,512]{1,0:T(8,128)(2,1)S(1)} %collective-permute-done.5.rest_0_, bf16[6,384,512]{2,1,0:T(8,128)(2,1)} %forward.1.rest_1_, ...), custom_call_target="tpu_custom_call" | custom-call | tf_op jit(solution)/shard_map/own/pallas_call | solution.py:202
  (25 shorter events, 0.2 us)
Async XLA Ops:
  2.6 4.4 %copy-start.3 = (s32[24,6]{0,1:T(8,128)S(1)}, s32[24,6]{0,1:T(8,128)}, u32[]{:S(2)}) copy-start(s32[24,6]{0,1:T(8,128)} %param.7) | copy-start | bytes 1732
  2.6 4.7 %copy-start.1 = (f32[24,16,512]{2,1,0:T(8,128)S(1)}, f32[24,16,512]{2,1,0:T(8,128)}, u32[]{:S(2)}) copy-start(f32[24,16,512]{2,1,0:T(8,128)} %param.5) | copy-start | bytes 2359300
  2.6 14.6 %copy-start.4 = (f32[6,3]{0,1:T(4,128)S(1)}, f32[6,3]{0,1:T(4,128)}, u32[]{:S(2)}) copy-start(f32[6,3]{0,1:T(4,128)} %param.8) | copy-start | bytes 220
  2.7 14.7 %copy-start.5 = (s32[6,3]{0,1:T(4,128)S(1)}, s32[6,3]{0,1:T(4,128)}, u32[]{:S(2)}) copy-start(s32[6,3]{0,1:T(4,128)} %param.9) | copy-start | bytes 220
  2.7 34.2 %all-to-all-start = ((bf16[4,18,16,512]{3,2,1,0:T(8,128)(2,1)}), bf16[4,18,16,512]{3,2,1,0:T(8,128)(2,1)S(1)}, u32[]{:S(2)}, u32[]{:S(2)}) async-start(bf16[4,18,16,512]{3,2,1,0:T(8,128)(2,1)} %get-tuple-element.22), calls=%async_computation | async-start | bytes 2359296 | tf_op jit(solution)/shard_map/all_to_all | solution.py:294
  8.1 33.3 %collective-permute-start = (bf16[400,512]{1,0:T(8,128)(2,1)}, bf16[400,512]{1,0:T(8,128)(2,1)S(1)}, u32[]{:S(2)}, u32[]{:S(2)}) collective-permute-start(bf16[400,512]{1,0:T(8,128)(2,1)} %pad_maximum_fusion), channel_id=1, source_target_pairs={{0,8},{1,9},{2,10},{3,11},{4,12},{5,13},{6,14},{7,15},{8,0},{9,1},... | collective-permute-start | bytes 1228808 | tf_op jit(solution)/shard_map/ppermute | solution.py:309
  11.5 30.6 %collective-permute-start.1 = (bf16[1,18,16,512]{3,2,1,0:T(8,128)(2,1)}, bf16[1,18,16,512]{3,2,1,0:T(8,128)(2,1)}, u32[]{:S(2)}, u32[]{:S(2)}) collective-permute-start(bf16[1,18,16,512]{3,2,1,0:T(8,128)(2,1)} %get-tuple-element.28), channel_id=1, source_target_pairs={{0,4},{1,5},{2,6},{3,7},{4,0},{5,1},{6,2},{7,3},{8,12},{9,13},{10,... | collective-permute-start | bytes 884744 | tf_op jit(solution)/shard_map/ppermute | solution.py:315
  13.0 29.1 %collective-permute-start.2 = (bf16[1,18,16,512]{3,2,1,0:T(8,128)(2,1)}, bf16[1,18,16,512]{3,2,1,0:T(8,128)(2,1)}, u32[]{:S(2)}, u32[]{:S(2)}) collective-permute-start(bf16[1,18,16,512]{3,2,1,0:T(8,128)(2,1)} %get-tuple-element.29), channel_id=1, source_target_pairs={{0,5},{1,6},{2,7},{3,4},{4,1},{5,2},{6,3},{7,0},{8,13},{9,14},{10,... | collective-permute-start | bytes 884744 | tf_op jit(solution)/shard_map/ppermute | solution.py:315
  13.0 30.3 %collective-permute-start.3 = (bf16[1,18,16,512]{3,2,1,0:T(8,128)(2,1)}, bf16[1,18,16,512]{3,2,1,0:T(8,128)(2,1)}, u32[]{:S(2)}, u32[]{:S(2)}) collective-permute-start(bf16[1,18,16,512]{3,2,1,0:T(8,128)(2,1)} %get-tuple-element.30), channel_id=1, source_target_pairs={{0,6},{1,7},{2,4},{3,5},{4,2},{5,3},{6,0},{7,1},{8,14},{9,15},{10,... | collective-permute-start | bytes 884744 | tf_op jit(solution)/shard_map/ppermute | solution.py:315
  15.7 31.2 %collective-permute-start.4 = (bf16[1,18,16,512]{3,2,1,0:T(8,128)(2,1)}, bf16[1,18,16,512]{3,2,1,0:T(8,128)(2,1)}, u32[]{:S(2)}, u32[]{:S(2)}) collective-permute-start(bf16[1,18,16,512]{3,2,1,0:T(8,128)(2,1)} %get-tuple-element.31), channel_id=1, source_target_pairs={{0,7},{1,4},{2,5},{3,6},{4,3},{5,0},{6,1},{7,2},{8,15},{9,12},{10,... | collective-permute-start | bytes 884744 | tf_op jit(solution)/shard_map/ppermute | solution.py:315
  27.7 1.9 %copy-start = (bf16[6,512,512]{2,1,0:T(8,128)(2,1)S(1)}, bf16[6,512,512]{2,1,0:T(8,128)(2,1)}, u32[]{:S(2)}) copy-start(bf16[6,512,512]{2,1,0:T(8,128)(2,1)} %get-tuple-element.21.wf.rest_0_) | copy-start | bytes 9437188
  36.8 1.0 %copy-start.2 = (bf16[4,18,16,512]{3,2,1,0:T(8,128)(2,1)}, bf16[4,18,16,512]{3,2,1,0:T(8,128)(2,1)S(1)}, u32[]{:S(2)}) copy-start(bf16[4,18,16,512]{3,2,1,0:T(8,128)(2,1)S(1)} %all-to-all-done) | copy-start | bytes 3538948
  37.8 43.3 %all-to-all-start.1 = ((bf16[8,18,16,512]{3,2,1,0:T(8,128)(2,1)}), bf16[8,18,16,512]{3,2,1,0:T(8,128)(2,1)S(1)}, u32[]{:S(2)}, u32[]{:S(2)}) async-start(bf16[8,18,16,512]{3,2,1,0:T(8,128)(2,1)} %pick_own.1), calls=%async_computation.1 | async-start | bytes 4718592 | tf_op jit(solution)/shard_map/all_to_all | solution.py:294
  54.4 25.8 %collective-permute-start.5 = (bf16[384,512]{1,0:T(8,128)(2,1)}, bf16[384,512]{1,0:T(8,128)(2,1)S(1)}, u32[]{:S(2)}, u32[]{:S(2)}) collective-permute-start(bf16[384,512]{1,0:T(8,128)(2,1)} %other.1), channel_id=1, source_target_pairs={{0,8},{1,9},{2,10},{3,11},{4,12},{5,13},{6,14},{7,15},{8,0},{9,1},... | collective-permute-start | bytes 1179656 | tf_op jit(solution)/shard_map/ppermute | solution.py:327

commit v5 on v4

--- a/solution.py
+++ b/solution.py
@@ -317,9 +317,8 @@
     matrices = _matrices(psf_sigma, view_offsets, depth, plane)
     rb_own = _forward(est_bf, matrices[0], matrices[2])
     slots_own = _slots(item_tile, mine * half, half, slot_count)
-    held, _ = lax.optimization_barrier((observed[0], matrices[2]))
+    held, obs_near = lax.optimization_barrier((observed[0], obs_near))
     (own,) = _pick(held, [half], lambda me, j: me // half * half + j, "pick_own")
-    own, rb_own, slots_own, obs_near = lax.optimization_barrier((own, rb_own, slots_own, obs_near))
     obs_own = exchange(own, halves)
     item_tile_other = est_other[blocks * depth :].reshape(-1)[: blocks * views].astype(jnp.int32).reshape(blocks, views)
     slots_other = _slots(item_tile_other, mine * half, half, slot_count, place)

time: 87.1 us -> 86.9 us (level)
  local copies, waits for them, and re-layouts: 3.84 us -> 2.27 us
  waiting for transfers between devices: 29.5 us -> 30.5 us
    ppermute x4, waiting for transfers between devices: 4.76 us -> 11.3 us  [per_device(): lax.ppermute(sent, 'tiles', ring).reshape(slot_count, depth, plane)]
    ppermute x1, waiting for transfers between devices: 23.8 us -> 18.1 us  [per_device(): product = lax.ppermute(sent_back, 'tiles', swap)]
    unnamed x17 -> x23, local copies, waits for them, and re-layouts: 3.18 us -> 1.62 us
  transfers between devices with their start and end apart: 8 -> 8, of which waited for: 4 -> 4; matrix products, arithmetic and copies ran while one was open for 3% -> 3% of each run, Pallas kernels for 28% -> 29%
where the time goes in v5:
time: 86.9 us; the launch traced here: 86.5 us
  Pallas kernels  33.6 us (39%)
  waiting for transfers between devices  30.5 us (35%)
  starting transfers between devices  19.4 us (22%)
  local copies, waits for them, and re-layouts  2.27 us (3%)
    ppermute x1, waiting for transfers between devices, per_device(): product = lax.ppermute(sent_back, 'tiles', swap)  18.1 us
    pallas_call x2, Pallas kernels, _call(): pl.pallas_call(kernel, in_specs=[smem] + [vmem] * len(whole) + [hbm] * le...  13.7 us
    ppermute x4, waiting for transfers between devices, per_device(): lax.ppermute(sent, 'tiles', ring).reshape(slot_count, depth, plane)  11.3 us
    pallas_call x1, Pallas kernels, _matrices(): pl.pallas_call(_matrices_kernel, grid=(views,), in_specs=[smem, smem], ou...  9.91 us
    all_to_all x2, starting transfers between devices, exchange(): lax.all_to_all(sent, 'tiles', 0, 0, axis_index_groups=groups, tiled=True)  8.01 us
    ppermute x4, starting transfers between devices, per_device(): lax.ppermute(sent, 'tiles', ring).reshape(slot_count, depth, plane)  5.81 us
    pallas_call x2, Pallas kernels, _pick(): pl.pallas_call(functools.partial(_pick_kernel, owners), in_specs=[hbm], o...  5.51 us
    pallas_call x1, Pallas kernels, _forward(): pl.pallas_call(_forward_kernel, grid=(views,), in_specs=[pl.BlockSpec((ro...  4.51 us
  transfers between devices with their start and end apart: 8, of which 4 were waited for; matrix products, arithmetic and copies ran while one was open for 3% of the time, Pallas kernels for 29%

profile of v5, /device:TPU:0, one launch (start us, length us, event | category | flops | bytes accessed | tf_op | source)
XLA Modules:
  0.0 86.5 jit_solution(9403017438294059164)
XLA Ops:
  0.0 2.5 %pick_other.1 = (bf16[4,18,16,512]{3,2,1,0:T(8,128)(2,1)}, bf16[1,18,16,512]{3,2,1,0:T(8,128)(2,1)}, bf16[1,18,16,512]{3,2,1,0:T(8,128)(2,1)}, bf16[1,18,16,512]{3,2,1,0:T(8,128)(2,1)}, bf16[1,18,16,512]{3,2,1,0:T(8,128)(2,1)}) custom-call(bf16[16,18,16,512]{3,2,1,0:T(8,128)(2,1)} %bitcast.18), custom_call_target="tpu_custom_call" | custom-call | tf_op jit(solution)/shard_map/pick_other/pallas_call | solution.py:257
  2.5 0.0 copy-start.1
  2.6 4.4 %all-to-all-start = ((bf16[4,18,16,512]{3,2,1,0:T(8,128)(2,1)}), bf16[4,18,16,512]{3,2,1,0:T(8,128)(2,1)S(1)}, u32[]{:S(2)}, u32[]{:S(2)}) async-start(bf16[4,18,16,512]{3,2,1,0:T(8,128)(2,1)} %get-tuple-element.17), calls=%async_computation | async-start | bytes 2359296 | tf_op jit(solution)/shard_map/all_to_all | solution.py:294
  6.9 0.1 copy.19
  7.0 0.1 eq.42
  7.1 0.6 copy-done.5
  7.8 3.4 %collective-permute-start = (bf16[400,512]{1,0:T(8,128)(2,1)S(1)}, bf16[400,512]{1,0:T(8,128)(2,1)}, u32[]{:S(2)}, u32[]{:S(2)}) collective-permute-start(bf16[400,512]{1,0:T(8,128)(2,1)S(1)} %pad_maximum_fusion), channel_id=1, source_target_pairs={{0,8},{1,9},{2,10},{3,11},{4,12},{5,13},{6,14},{7,15},{8,0},{9,1},... | collective-permute-start | bytes 1228808 | tf_op jit(solution)/shard_map/ppermute | solution.py:309
  11.3 1.6 %collective-permute-start.1 = (bf16[1,18,16,512]{3,2,1,0:T(8,128)(2,1)}, bf16[1,18,16,512]{3,2,1,0:T(8,128)(2,1)}, u32[]{:S(2)}, u32[]{:S(2)}) collective-permute-start(bf16[1,18,16,512]{3,2,1,0:T(8,128)(2,1)} %get-tuple-element.23), channel_id=1, source_target_pairs={{0,4},{1,5},{2,6},{3,7},{4,0},{5,1},{6,2},{7,3},{8,12},{9,13},{10,... | collective-permute-start | bytes 884744 | tf_op jit(solution)/shard_map/ppermute | solution.py:315
  12.8 2.6 %collective-permute-start.3 = (bf16[1,18,16,512]{3,2,1,0:T(8,128)(2,1)}, bf16[1,18,16,512]{3,2,1,0:T(8,128)(2,1)}, u32[]{:S(2)}, u32[]{:S(2)}) collective-permute-start(bf16[1,18,16,512]{3,2,1,0:T(8,128)(2,1)} %get-tuple-element.25), channel_id=1, source_target_pairs={{0,6},{1,7},{2,4},{3,5},{4,2},{5,3},{6,0},{7,1},{8,14},{9,15},{10,... | collective-permute-start | bytes 884744 | tf_op jit(solution)/shard_map/ppermute | solution.py:315
  15.5 1.6 %collective-permute-start.4 = (bf16[1,18,16,512]{3,2,1,0:T(8,128)(2,1)}, bf16[1,18,16,512]{3,2,1,0:T(8,128)(2,1)}, u32[]{:S(2)}, u32[]{:S(2)}) collective-permute-start(bf16[1,18,16,512]{3,2,1,0:T(8,128)(2,1)} %get-tuple-element.26), channel_id=1, source_target_pairs={{0,7},{1,4},{2,5},{3,6},{4,3},{5,0},{6,1},{7,2},{8,15},{9,12},{10,... | collective-permute-start | bytes 884744 | tf_op jit(solution)/shard_map/ppermute | solution.py:315
  17.1 0.1 copy.21.sigma
  17.2 0.1 copy.22.offset
  17.3 9.9 %matrices.1 = (bf16[6,512,512]{2,1,0:T(8,128)(2,1)}, bf16[6,512,512]{2,1,0:T(8,128)(2,1)}, bf16[6,128,128]{2,1,0:T(8,128)(2,1)S(1)}, bf16[6,128,128]{2,1,0:T(8,128)(2,1)S(1)}) custom-call(f32[6,3]{1,0:T(8,128)S(1)} %copy.21.sigma, s32[6,3]{1,0:T(8,128)S(1)} %copy.22.offset), custom_call_target="tpu_custom_call" | custom-call | tf_op jit(solution)/shard_map/matrices/pallas_call | solution.py:58
  27.2 3.0 %pick_own.1 = bf16[8,18,16,512]{3,2,1,0:T(8,128)(2,1)} custom-call(bf16[16,18,16,512]{3,2,1,0:T(8,128)(2,1)} %bitcast.19), custom_call_target="tpu_custom_call" | custom-call | tf_op jit(solution)/shard_map/pick_own/pallas_call | solution.py:257
  30.2 3.6 %all-to-all-start.1 = ((bf16[8,18,16,512]{3,2,1,0:T(8,128)(2,1)}), bf16[8,18,16,512]{3,2,1,0:T(8,128)(2,1)S(1)}, u32[]{:S(2)}, u32[]{:S(2)}) async-start(bf16[8,18,16,512]{3,2,1,0:T(8,128)(2,1)} %pick_own.1), calls=%async_computation.1 | async-start | bytes 4718592 | tf_op jit(solution)/shard_map/all_to_all | solution.py:294
  33.8 0.7 slice_bitcast_fusion
  34.6 0.1 sub.42
  34.7 0.1 copy.23
  34.8 0.2 convert_reduce_fusion
  35.0 0.1 reduce_sum.25
  35.1 0.1 copy.29
  35.2 8.0 %collective-permute-done.3 = bf16[1,18,16,512]{3,2,1,0:T(8,128)(2,1)} collective-permute-done((bf16[1,18,16,512]{3,2,1,0:T(8,128)(2,1)}, bf16[1,18,16,512]{3,2,1,0:T(8,128)(2,1)}, u32[]{:S(2)}, u32[]{:S(2)}) %collective-permute-start.3) | collective-permute-done | bytes 294944 | tf_op jit(solution)/shard_map/ppermute | solution.py:315
  43.2 3.3 %collective-permute-done.4 = bf16[1,18,16,512]{3,2,1,0:T(8,128)(2,1)} collective-permute-done((bf16[1,18,16,512]{3,2,1,0:T(8,128)(2,1)}, bf16[1,18,16,512]{3,2,1,0:T(8,128)(2,1)}, u32[]{:S(2)}, u32[]{:S(2)}) %collective-permute-start.4) | collective-permute-done | bytes 294944 | tf_op jit(solution)/shard_map/ppermute | solution.py:315
  46.5 8.1 %other.1 = bf16[384,512]{1,0:T(8,128)(2,1)} custom-call(s32[6,24]{1,0:T(8,128)S(1)} %fusion.9.slots, bf16[400,512]{1,0:T(8,128)(2,1)} %collective-permute-done.est, bf16[6,128,128]{2,1,0:T(8,128)(2,1)S(1)} %get-tuple-element.19.zf, bf16[6,128,128]{2,1,0:T(8,128)(2,1)S(1)} %get-tuple-element.16.zb, bf16[6,512,512]{2,1,0:T(8,128)(2,1)} %get-tuple-element.20.rest_0_.wf, ...), custom_call_target="tpu_custom_call" | custom-call | flops 30000001024 | bytes 104857600 | tf_op jit(solution)/shard_map/other/pallas_call | solution.py:202
  54.6 2.2 %collective-permute-start.5 = (bf16[384,512]{1,0:T(8,128)(2,1)}, bf16[384,512]{1,0:T(8,128)(2,1)S(1)}, u32[]{:S(2)}, u32[]{:S(2)}) collective-permute-start(bf16[384,512]{1,0:T(8,128)(2,1)} %other.1), channel_id=1, source_target_pairs={{0,8},{1,9},{2,10},{3,11},{4,12},{5,13},{6,14},{7,15},{8,0},{9,1},... | collective-permute-start | bytes 1179656 | tf_op jit(solution)/shard_map/ppermute | solution.py:326
  56.8 4.5 %forward.1.rest_1_ = bf16[6,384,512]{2,1,0:T(8,128)(2,1)} custom-call(bf16[384,512]{1,0:T(8,128)(2,1)S(1)} %bitcast_convert_fusion.est, bf16[6,512,512]{2,1,0:T(8,128)(2,1)S(1)} %copy-done, bf16[6,128,128]{2,1,0:T(8,128)(2,1)S(1)} %get-tuple-element.19.zf), custom_call_target="tpu_custom_call" | custom-call | tf_op jit(solution)/shard_map/forward/pallas_call | solution.py:90
  61.3 0.2 convert_reduce_fusion.1
  61.5 0.1 reduce_sum.23
  61.6 0.1 copy.20
  61.7 18.1 %collective-permute-done.5.rest_0_ = bf16[384,512]{1,0:T(8,128)(2,1)S(1)} collective-permute-done((bf16[384,512]{1,0:T(8,128)(2,1)}, bf16[384,512]{1,0:T(8,128)(2,1)S(1)}, u32[]{:S(2)}, u32[]{:S(2)}) %collective-permute-start.5) | collective-permute-done | bytes 393248 | tf_op jit(solution)/shard_map/ppermute | solution.py:326
  79.8 1.1 %all-to-all-done.1 = bf16[8,18,16,512]{3,2,1,0:T(8,128)(2,1)S(1)} async-done(((bf16[8,18,16,512]{3,2,1,0:T(8,128)(2,1)}), bf16[8,18,16,512]{3,2,1,0:T(8,128)(2,1)S(1)}, u32[]{:S(2)}, u32[]{:S(2)}) %all-to-all-start.1) | async-done | bytes 2359328 | tf_op jit(solution)/shard_map/all_to_all | solution.py:294
  80.9 5.7 %own.1 = f32[384,512]{1,0:T(8,128)} custom-call(s32[6,24]{1,0:T(8,128)S(1)} %select_bitcast_fusion.slots, bf16[6,128,128]{2,1,0:T(8,128)(2,1)S(1)} %get-tuple-element.16.zb, bf16[144,16,512]{2,1,0:T(8,128)(2,1)S(1)} %bitcast.17, bf16[384,512]{1,0:T(8,128)(2,1)S(1)} %collective-permute-done.5.rest_0_, bf16[6,384,512]{2,1,0:T(8,128)(2,1)} %forward.1.rest_1_, ...), custom_call_target="tpu_custom_call" | custom-call | tf_op jit(solution)/shard_map/own/pallas_call | solution.py:202
  (31 shorter events, 0.2 us)
Async XLA Ops:
  2.5 4.4 %copy-start.3 = (s32[24,6]{0,1:T(8,128)S(1)}, s32[24,6]{0,1:T(8,128)}, u32[]{:S(2)}) copy-start(s32[24,6]{0,1:T(8,128)} %param.7) | copy-start | bytes 1732
  2.5 5.2 %copy-start.1 = (f32[24,16,512]{2,1,0:T(8,128)S(1)}, f32[24,16,512]{2,1,0:T(8,128)}, u32[]{:S(2)}) copy-start(f32[24,16,512]{2,1,0:T(8,128)} %param.5) | copy-start | bytes 2359300
  2.5 14.5 %copy-start.7 = (f32[6,3]{0,1:T(4,128)S(1)}, f32[6,3]{0,1:T(4,128)}, u32[]{:S(2)}) copy-start(f32[6,3]{0,1:T(4,128)} %param.8) | copy-start | bytes 220
  2.5 14.6 %copy-start.8 = (s32[6,3]{0,1:T(4,128)S(1)}, s32[6,3]{0,1:T(4,128)}, u32[]{:S(2)}) copy-start(s32[6,3]{0,1:T(4,128)} %param.9) | copy-start | bytes 220
  2.6 24.6 %all-to-all-start = ((bf16[4,18,16,512]{3,2,1,0:T(8,128)(2,1)}), bf16[4,18,16,512]{3,2,1,0:T(8,128)(2,1)S(1)}, u32[]{:S(2)}, u32[]{:S(2)}) async-start(bf16[4,18,16,512]{3,2,1,0:T(8,128)(2,1)} %get-tuple-element.17), calls=%async_computation | async-start | bytes 2359296 | tf_op jit(solution)/shard_map/all_to_all | solution.py:294
  7.1 0.6 copy-start.5
  7.8 26.0 %collective-permute-start = (bf16[400,512]{1,0:T(8,128)(2,1)S(1)}, bf16[400,512]{1,0:T(8,128)(2,1)}, u32[]{:S(2)}, u32[]{:S(2)}) collective-permute-start(bf16[400,512]{1,0:T(8,128)(2,1)S(1)} %pad_maximum_fusion), channel_id=1, source_target_pairs={{0,8},{1,9},{2,10},{3,11},{4,12},{5,13},{6,14},{7,15},{8,0},{9,1},... | collective-permute-start | bytes 1228808 | tf_op jit(solution)/shard_map/ppermute | solution.py:309
  11.3 23.9 %collective-permute-start.1 = (bf16[1,18,16,512]{3,2,1,0:T(8,128)(2,1)}, bf16[1,18,16,512]{3,2,1,0:T(8,128)(2,1)}, u32[]{:S(2)}, u32[]{:S(2)}) collective-permute-start(bf16[1,18,16,512]{3,2,1,0:T(8,128)(2,1)} %get-tuple-element.23), channel_id=1, source_target_pairs={{0,4},{1,5},{2,6},{3,7},{4,0},{5,1},{6,2},{7,3},{8,12},{9,13},{10,... | collective-permute-start | bytes 884744 | tf_op jit(solution)/shard_map/ppermute | solution.py:315
  12.8 22.4 %collective-permute-start.2 = (bf16[1,18,16,512]{3,2,1,0:T(8,128)(2,1)}, bf16[1,18,16,512]{3,2,1,0:T(8,128)(2,1)}, u32[]{:S(2)}, u32[]{:S(2)}) collective-permute-start(bf16[1,18,16,512]{3,2,1,0:T(8,128)(2,1)} %get-tuple-element.24), channel_id=1, source_target_pairs={{0,5},{1,6},{2,7},{3,4},{4,1},{5,2},{6,3},{7,0},{8,13},{9,14},{10,... | collective-permute-start | bytes 884744 | tf_op jit(solution)/shard_map/ppermute | solution.py:315
  12.8 30.3 %collective-permute-start.3 = (bf16[1,18,16,512]{3,2,1,0:T(8,128)(2,1)}, bf16[1,18,16,512]{3,2,1,0:T(8,128)(2,1)}, u32[]{:S(2)}, u32[]{:S(2)}) collective-permute-start(bf16[1,18,16,512]{3,2,1,0:T(8,128)(2,1)} %get-tuple-element.25), channel_id=1, source_target_pairs={{0,6},{1,7},{2,4},{3,5},{4,2},{5,3},{6,0},{7,1},{8,14},{9,15},{10,... | collective-permute-start | bytes 884744 | tf_op jit(solution)/shard_map/ppermute | solution.py:315
  15.5 31.1 %collective-permute-start.4 = (bf16[1,18,16,512]{3,2,1,0:T(8,128)(2,1)}, bf16[1,18,16,512]{3,2,1,0:T(8,128)(2,1)}, u32[]{:S(2)}, u32[]{:S(2)}) collective-permute-start(bf16[1,18,16,512]{3,2,1,0:T(8,128)(2,1)} %get-tuple-element.26), channel_id=1, source_target_pairs={{0,7},{1,4},{2,5},{3,6},{4,3},{5,0},{6,1},{7,2},{8,15},{9,12},{10,... | collective-permute-start | bytes 884744 | tf_op jit(solution)/shard_map/ppermute | solution.py:315
  27.2 3.0 %copy-start.2 = (bf16[4,18,16,512]{3,2,1,0:T(8,128)(2,1)}, bf16[4,18,16,512]{3,2,1,0:T(8,128)(2,1)S(1)}, u32[]{:S(2)}) copy-start(bf16[4,18,16,512]{3,2,1,0:T(8,128)(2,1)S(1)} %all-to-all-done) | copy-start | bytes 3538948
  30.2 50.7 %all-to-all-start.1 = ((bf16[8,18,16,512]{3,2,1,0:T(8,128)(2,1)}), bf16[8,18,16,512]{3,2,1,0:T(8,128)(2,1)S(1)}, u32[]{:S(2)}, u32[]{:S(2)}) async-start(bf16[8,18,16,512]{3,2,1,0:T(8,128)(2,1)} %pick_own.1), calls=%async_computation.1 | async-start | bytes 4718592 | tf_op jit(solution)/shard_map/all_to_all | solution.py:294
  46.5 10.3 %copy-start = (bf16[6,512,512]{2,1,0:T(8,128)(2,1)S(1)}, bf16[6,512,512]{2,1,0:T(8,128)(2,1)}, u32[]{:S(2)}) copy-start(bf16[6,512,512]{2,1,0:T(8,128)(2,1)} %get-tuple-element.20.rest_0_.wf) | copy-start | bytes 9437188
  54.6 6.7 %copy-start.6 = (s32[144]{0:T(256)S(1)}, s32[144]{0:T(256)}, u32[]{:S(2)}) copy-start(s32[144]{0:T(256)} %copy-done.5) | copy-start | bytes 1732
  54.6 7.1 %copy-start.4 = (s32[24,6]{0,1:T(8,128)S(1)}, s32[24,6]{0,1:T(8,128)}, u32[]{:S(2)}) copy-start(s32[24,6]{0,1:T(8,128)} %param.7) | copy-start | bytes 1732
  54.6 25.2 %collective-permute-start.5 = (bf16[384,512]{1,0:T(8,128)(2,1)}, bf16[384,512]{1,0:T(8,128)(2,1)S(1)}, u32[]{:S(2)}, u32[]{:S(2)}) collective-permute-start(bf16[384,512]{1,0:T(8,128)(2,1)} %other.1), channel_id=1, source_target_pairs={{0,8},{1,9},{2,10},{3,11},{4,12},{5,13},{6,14},{7,15},{8,0},{9,1},... | collective-permute-start | bytes 1179656 | tf_op jit(solution)/shard_map/ppermute | solution.py:326
